TPU v7x, 32 devices: a whole 2x2x4 slice. The times are simulated.
32 devices in a mesh: patch: 16 (over z, x, core), sample: 2 (over y).
Axes of the slice: x: 2, y: 2, z: 4, core: 2. Of those that a mesh axis runs over, the one named last changes fastest.
Arguments:
- nodes: bfloat16 [8, 8192, 512], P('sample', 'patch'), may hold values from -6 to 6
- neighbours: int32 [8192, 16], P('patch'), may hold values from 0 to 767
- send_rows: int32 [64, 64], P('patch'), may hold values from 0 to 511
- noise_code: float32 [8, 16], P('sample'), may hold values from -5 to 5
- w_query: bfloat16 [512, 512], P(('patch', 'sample')), may hold values from -0.25 to 0.25
- w_key: bfloat16 [512, 512], P(('patch', 'sample')), may hold values from -0.25 to 0.25
- w_value: bfloat16 [512, 512], P(('patch', 'sample')), may hold values from -0.25 to 0.25
- w_out: bfloat16 [512, 512], P(('patch', 'sample')), may hold values from -0.5 to 0.5
- w_up: bfloat16 [512, 2048], P(('patch', 'sample')), may hold values from -0.25 to 0.25
- b_up: bfloat16 [2048], P(('patch', 'sample')), may hold values from -3 to 3
- w_down: bfloat16 [2048, 512], P(('patch', 'sample')), may hold values from -0.1875 to 0.1875
- b_down: bfloat16 [512], P(('patch', 'sample')), may hold values from -3 to 3
- cond_weight: bfloat16 [16, 2048], P(None, ('patch', 'sample')), may hold values from -1 to 1
- cond_bias: bfloat16 [2048], P(('patch', 'sample')), may hold values from -2 to 2
- cotangent: bfloat16 [8, 8192, 512], P('sample', 'patch'), may hold values from -6 to 6
Outputs:
- out_nodes: bfloat16 [8, 8192, 512], P('sample', 'patch')
- grad_nodes: float32 [8, 8192, 512], P('sample', 'patch')
- grad_query: float32 [512, 512], P(('patch', 'sample'))
- grad_key: float32 [512, 512], P(('patch', 'sample'))
- grad_value: float32 [512, 512], P(('patch', 'sample'))
- grad_out: float32 [512, 512], P(('patch', 'sample'))
- grad_up: float32 [512, 2048], P(('patch', 'sample'))
- grad_b_up: float32 [2048], P(('patch', 'sample'))
- grad_down: float32 [2048, 512], P(('patch', 'sample'))
- grad_b_down: float32 [512], P(('patch', 'sample'))
- grad_cond_weight: float32 [16, 2048], P(None, ('patch', 'sample'))
- grad_cond_bias: float32 [2048], P(('patch', 'sample'))
Inputs may be any that keep to these rules, and one draw needn't show every extreme that they name: `send_rows`: row 4 q + b lists local node numbers of patch q; repeats are allowed.
All inputs are finite; a program needn't handle non-finite values.
Results may differ from a plain program's by a relative error of at most 0.014.
The roundings to bfloat16 on the way count: a program that leaves them out, or rounds other values in their place, can miss the bound.
Values may be sent and summed in bfloat16 or wider, within the bound.
No kernel may reach another device: no remote copies, remote signals or barrier semaphores. Data moves between devices by JAX's collectives and lax.ppermute only.
A program may use at most 320 MiB of HBM per device.

v0:
```python
import jax
import jax.numpy as jnp
from jax import lax
from jax.sharding import PartitionSpec as P

HEAD = 128
STRIDE = 4


epsilon = 1e-05


def from_behind(block, axis, distance):
    devices = range(lax.axis_size(axis))
    route = [((i - distance) % len(devices), i) for i in devices]
    return lax.ppermute(block, axis, route)


def product(left_operand, right_operand):
    return jnp.dot(left_operand, right_operand, preferred_element_type=jnp.float32)


def layer_normalize(values):
    centre = jnp.mean(values, axis=-1, keepdims=True)
    centred = values - centre
    inverse = lax.rsqrt(jnp.mean(centred * centred, axis=-1, keepdims=True) + epsilon)
    return (centred * inverse, inverse)


def norm_back(grad_hat, normed, inverse):
    first = jnp.mean(grad_hat, axis=-1, keepdims=True)
    second = jnp.mean(grad_hat * normed, axis=-1, keepdims=True)
    return inverse * (grad_hat - first - normed * second)


def body(
    nodes,
    neighbours,
    send_rows,
    noise_code,
    w_query,
    w_key,
    w_value,
    w_out,
    w_up,
    b_up,
    w_down,
    b_down,
    cond_weight,
    cond_bias,
    cotangent,
):
    (
        full_query,
        full_key,
        full_value,
        full_out,
        full_up,
        full_bias_up,
        full_down,
        full_bias_down,
        complete_conditioning,
        full_cond_bias,
    ) = (
        lax.all_gather(w_query, ("patch", "sample"), axis=0, tiled=True),
        lax.all_gather(w_key, ("patch", "sample"), axis=0, tiled=True),
        lax.all_gather(w_value, ("patch", "sample"), axis=0, tiled=True),
        lax.all_gather(w_out, ("patch", "sample"), axis=0, tiled=True),
        lax.all_gather(w_up, ("patch", "sample"), axis=0, tiled=True),
        lax.all_gather(b_up, ("patch", "sample"), axis=0, tiled=True),
        lax.all_gather(w_down, ("patch", "sample"), axis=0, tiled=True),
        lax.all_gather(b_down, ("patch", "sample"), axis=0, tiled=True),
        lax.all_gather(cond_weight, ("patch", "sample"), axis=1, tiled=True),
        lax.all_gather(cond_bias, ("patch", "sample"), axis=0, tiled=True),
    )
    samples, count, width = nodes.shape
    heads = width // HEAD
    rows = samples * count
    halo_rows = send_rows.shape[1]
    table = count + 4 * halo_rows
    offsets = (1, -1, STRIDE, -STRIDE)
    inv_root = HEAD ** (-0.5)
    modulate = jnp.dot(
        noise_code, complete_conditioning.astype(jnp.float32), precision=lax.Precision.HIGHEST
    ) + full_cond_bias.astype(jnp.float32)
    scale_one = 1.0 + modulate[:, None, 0:width]
    shift_one = modulate[:, None, width : 2 * width]
    scale_two = 1.0 + modulate[:, None, 2 * width : 3 * width]
    shift_two = modulate[:, None, 3 * width :]
    inputs = nodes.astype(jnp.float32)
    hat_one, inv_one = layer_normalize(inputs)
    act_one = (hat_one * scale_one + shift_one).astype(jnp.bfloat16).reshape(rows, width)
    queries = product(act_one, full_query).astype(jnp.bfloat16)
    keys = product(act_one, full_key).astype(jnp.bfloat16).reshape(samples, count, width)
    values = product(act_one, full_value).astype(jnp.bfloat16).reshape(samples, count, width)
    key_blocks = [keys]
    value_blocks = [values]
    for direction in range(4):
        picked = send_rows[direction]
        got_keys, got_values = from_behind(
            (keys[:, picked], values[:, picked]), "patch", offsets[direction]
        )
        key_blocks.append(got_keys)
        value_blocks.append(got_values)
    key_table = jnp.concatenate(key_blocks, axis=1)
    value_table = jnp.concatenate(value_blocks, axis=1)
    query_heads = queries.reshape(samples, count, heads, HEAD)
    key_near = key_table[:, neighbours].reshape(samples, count, -1, heads, HEAD)
    value_near = value_table[:, neighbours].reshape(samples, count, -1, heads, HEAD)
    scores = (
        jnp.einsum("snhd,snkhd->snhk", query_heads, key_near, preferred_element_type=jnp.float32)
        * inv_root
    )
    top_score = jnp.max(scores, axis=-1, keepdims=True)
    expo = jnp.exp(scores - top_score)
    total = jnp.sum(expo, axis=-1, keepdims=True)
    probs = expo / total
    log_total = top_score + jnp.log(total)
    probs_low = probs.astype(jnp.bfloat16)
    attended = jnp.einsum(
        "snhk,snkhd->snhd", probs_low, value_near, preferred_element_type=jnp.float32
    )
    attended = attended.astype(jnp.bfloat16).reshape(rows, width)
    middle = inputs + product(attended, full_out).reshape(samples, count, width)
    hat_two, inv_two = layer_normalize(middle)
    act_two = (hat_two * scale_two + shift_two).astype(jnp.bfloat16).reshape(rows, width)
    pre_act = product(act_two, full_up) + full_bias_up.astype(jnp.float32)
    sigma_gate = jax.nn.sigmoid(pre_act)
    hidden = (pre_act * sigma_gate).astype(jnp.bfloat16)
    result = (
        middle
        + product(hidden, full_down).reshape(samples, count, width)
        + full_bias_down.astype(jnp.float32)
    )
    result = result.astype(jnp.bfloat16)
    grad_rows = cotangent.reshape(rows, width)
    grad_float = grad_rows.astype(jnp.float32)
    grad_down = product(hidden.T, grad_rows)
    grad_bias_down = jnp.sum(grad_float, axis=0)
    grad_hidden = product(grad_rows, full_down.T)
    grad_pre = (grad_hidden * (sigma_gate + pre_act * sigma_gate * (1.0 - sigma_gate))).astype(
        jnp.bfloat16
    )
    grad_up = product(act_two.T, grad_pre)
    grad_bias_up = jnp.sum(grad_pre.astype(jnp.float32), axis=0)
    grad_act_two = product(grad_pre, full_up.T).reshape(samples, count, width)
    grad_scale_two = jnp.sum(grad_act_two * hat_two, axis=1)
    grad_shift_two = jnp.sum(grad_act_two, axis=1)
    grad_middle = grad_float.reshape(samples, count, width) + norm_back(
        grad_act_two * scale_two, hat_two, inv_two
    )
    grad_branch = grad_middle.reshape(rows, width).astype(jnp.bfloat16)
    grad_out_proj = product(attended.T, grad_branch)
    grad_attended = (
        product(grad_branch, full_out.T).astype(jnp.bfloat16).reshape(samples, count, heads, HEAD)
    )
    recomputed_key_rows = [keys]
    again_values = [values]
    for direction in range(4):
        picked = send_rows[direction]
        new_keys, new_values = from_behind(
            (keys[:, picked], values[:, picked]), "patch", offsets[direction]
        )
        recomputed_key_rows.append(new_keys)
        again_values.append(new_values)
    key_table = jnp.concatenate(recomputed_key_rows, axis=1)
    value_table = jnp.concatenate(again_values, axis=1)
    key_near = key_table[:, neighbours].reshape(samples, count, -1, heads, HEAD)
    value_near = value_table[:, neighbours].reshape(samples, count, -1, heads, HEAD)
    scores = (
        jnp.einsum("snhd,snkhd->snhk", query_heads, key_near, preferred_element_type=jnp.float32)
        * inv_root
    )
    probs = jnp.exp(scores - log_total)
    probs_low = probs.astype(jnp.bfloat16)
    grad_probs = jnp.einsum(
        "snhd,snkhd->snhk", grad_attended, value_near, preferred_element_type=jnp.float32
    )
    grad_value_near = jnp.einsum(
        "snhk,snhd->snkhd", probs_low, grad_attended, preferred_element_type=jnp.float32
    )
    grad_scores = (
        probs * (grad_probs - jnp.sum(probs * grad_probs, axis=-1, keepdims=True))
    ).astype(jnp.bfloat16)
    grad_queries = (
        jnp.einsum("snhk,snkhd->snhd", grad_scores, key_near, preferred_element_type=jnp.float32)
        * inv_root
    )
    grad_queries = grad_queries.astype(jnp.bfloat16).reshape(rows, width)
    grad_key_near = (
        jnp.einsum("snhk,snhd->snkhd", grad_scores, query_heads, preferred_element_type=jnp.float32)
        * inv_root
    )
    slots = (
        neighbours[None, :, :] + (jnp.arange(samples, dtype=jnp.int32) * table)[:, None, None]
    ).reshape(-1)
    grad_key_table = jax.ops.segment_sum(
        grad_key_near.reshape(-1, width), slots, num_segments=samples * table
    ).reshape(samples, table, width)
    grad_value_table = jax.ops.segment_sum(
        grad_value_near.reshape(-1, width), slots, num_segments=samples * table
    ).reshape(samples, table, width)
    grad_keys = grad_key_table[:, :count]
    grad_values = grad_value_table[:, :count]
    for direction in range(4):
        begin = count + direction * halo_rows
        back_keys, back_values = (
            from_behind(
                grad_key_table[:, begin : begin + halo_rows].astype(jnp.bfloat16),
                "patch",
                -offsets[direction],
            ).astype(jnp.float32),
            from_behind(
                grad_value_table[:, begin : begin + halo_rows].astype(jnp.bfloat16),
                "patch",
                -offsets[direction],
            ).astype(jnp.float32),
        )
        picked = send_rows[direction]
        grad_keys = grad_keys.at[:, picked].add(back_keys)
        grad_values = grad_values.at[:, picked].add(back_values)
    grad_keys = grad_keys.astype(jnp.bfloat16).reshape(rows, width)
    grad_values = grad_values.astype(jnp.bfloat16).reshape(rows, width)
    grad_query = product(act_one.T, grad_queries)
    grad_key = product(act_one.T, grad_keys)
    grad_value = product(act_one.T, grad_values)
    grad_act_one = (
        product(grad_queries, full_query.T)
        + product(grad_keys, full_key.T)
        + product(grad_values, full_value.T)
    )
    grad_act_one = grad_act_one.reshape(samples, count, width)
    grad_scale_one = jnp.sum(grad_act_one * hat_one, axis=1)
    grad_shift_one = jnp.sum(grad_act_one, axis=1)
    grad_nodes = grad_middle + norm_back(grad_act_one * scale_one, hat_one, inv_one)
    grad_modulate = jnp.concatenate(
        [grad_scale_one, grad_shift_one, grad_scale_two, grad_shift_two], axis=1
    )
    grad_cond = jnp.dot(noise_code.T, grad_modulate, precision=lax.Precision.HIGHEST)
    grad_cond_bias = jnp.sum(grad_modulate, axis=0)
    (
        sum_query,
        sum_key,
        sum_value,
        sum_out,
        sum_up,
        sum_bias_up,
        sum_down,
        sum_bias_down,
        sum_cond,
        sum_cond_bias,
    ) = (
        lax.psum_scatter(grad_query, ("patch", "sample"), scatter_dimension=0, tiled=True),
        lax.psum_scatter(grad_key, ("patch", "sample"), scatter_dimension=0, tiled=True),
        lax.psum_scatter(grad_value, ("patch", "sample"), scatter_dimension=0, tiled=True),
        lax.psum_scatter(grad_out_proj, ("patch", "sample"), scatter_dimension=0, tiled=True),
        lax.psum_scatter(grad_up, ("patch", "sample"), scatter_dimension=0, tiled=True),
        lax.psum_scatter(grad_bias_up, ("patch", "sample"), scatter_dimension=0, tiled=True),
        lax.psum_scatter(grad_down, ("patch", "sample"), scatter_dimension=0, tiled=True),
        lax.psum_scatter(grad_bias_down, ("patch", "sample"), scatter_dimension=0, tiled=True),
        lax.psum_scatter(grad_cond, ("patch", "sample"), scatter_dimension=1, tiled=True),
        lax.psum_scatter(grad_cond_bias, ("patch", "sample"), scatter_dimension=0, tiled=True),
    )
    return (
        result,
        grad_nodes,
        sum_query,
        sum_key,
        sum_value,
        sum_out,
        sum_up,
        sum_bias_up,
        sum_down,
        sum_bias_down,
        sum_cond,
        sum_cond_bias,
    )


def solution(mesh):
    return jax.shard_map(
        body,
        mesh=mesh,
        in_specs=(
            P("sample", "patch", None),
            P("patch", None),
            P("patch", None),
            P("sample", None),
            P(("patch", "sample"), None),
            P(("patch", "sample"), None),
            P(("patch", "sample"), None),
            P(("patch", "sample"), None),
            P(("patch", "sample"), None),
            P(("patch", "sample")),
            P(("patch", "sample"), None),
            P(("patch", "sample")),
            P(None, ("patch", "sample")),
            P(("patch", "sample")),
            P("sample", "patch", None),
        ),
        out_specs=(
            P("sample", "patch", None),
            P("sample", "patch", None),
            P(("patch", "sample"), None),
            P(("patch", "sample"), None),
            P(("patch", "sample"), None),
            P(("patch", "sample"), None),
            P(("patch", "sample"), None),
            P(("patch", "sample")),
            P(("patch", "sample"), None),
            P(("patch", "sample")),
            P(None, ("patch", "sample")),
            P(("patch", "sample")),
        ),
        check_vma=False,
    )
```

profile of v0, /device:TPU:0, one launch (start us, length us, event | category | flops | bytes accessed | tf_op | source)
XLA Modules:
  0.0 2676.5 jit_solution(4755110640621778727)
XLA Ops:
  11.4 42.3 %all-reduce.7 = (bf16[2048]{0:T(1024)(128)(2,1)S(1)}, bf16[2048]{0:T(1024)(128)(2,1)S(1)}, bf16[512]{0:T(512)(128)(2,1)}) all-reduce(bf16[2048]{0:T(1024)(128)(2,1)S(1)} %dynamic-update-slice, bf16[2048]{0:T(1024)(128)(2,1)S(1)} %dynamic-update-slice.1, ...), channel_id=1, replica_groups=mesh['patch'=16,'sample'=2] {'patch','sample'}, use_global_device_ids=true, to_apply=%add | all-reduce | flops 4608 | bytes 18432
  53.7 67.2 %all-gather = bf16[32,64,16]{1,2,0:T(8,128)(2,1)S(1)} all-gather(bf16[1,64,16]{1,2,0:T(8,128)(2,1)} %bitcast.237), channel_id=1, replica_groups=mesh['patch'=16,'sample'=2] {'patch','sample'}, dimensions={0}, use_global_device_ids=true | all-gather | bytes 67584 | tf_op jit(solution)/shard_map/all_gather | solution.py:73
  124.9 66.2 %all_gather.33 = bf16[512,512]{1,0:T(8,128)(2,1)S(1)} all-gather(bf16[16,512]{1,0:T(8,128)(2,1)S(1)} %copy-done.52), channel_id=1, replica_groups=mesh['patch'=16,'sample'=2] {'patch','sample'}, dimensions={0}, use_global_device_ids=true | all-gather | bytes 540672 | tf_op jit(solution)/shard_map/all_gather | solution.py:66
  210.6 68.7 %all_gather.34 = bf16[512,512]{1,0:T(8,128)(2,1)S(1)} all-gather(bf16[16,512]{1,0:T(8,128)(2,1)S(1)} %copy-done.53), channel_id=1, replica_groups=mesh['patch'=16,'sample'=2] {'patch','sample'}, dimensions={0}, use_global_device_ids=true | all-gather | bytes 540672 | tf_op jit(solution)/shard_map/all_gather | solution.py:67
  308.5 68.6 %all_gather.32 = bf16[512,512]{1,0:T(8,128)(2,1)S(1)} all-gather(bf16[16,512]{1,0:T(8,128)(2,1)S(1)} %copy-done.54), channel_id=1, replica_groups=mesh['patch'=16,'sample'=2] {'patch','sample'}, dimensions={0}, use_global_device_ids=true | all-gather | bytes 540672 | tf_op jit(solution)/shard_map/all_gather | solution.py:65
  377.1 71.3 %all_gather.35 = bf16[512,512]{1,0:T(8,128)(2,1)} all-gather(bf16[16,512]{1,0:T(8,128)(2,1)S(1)} %copy-done.55), channel_id=1, replica_groups=mesh['patch'=16,'sample'=2] {'patch','sample'}, dimensions={0}, use_global_device_ids=true | all-gather | bytes 540672 | tf_op jit(solution)/shard_map/all_gather | solution.py:68
  502.0 84.5 %gather_fusion.9 = bf16[8192,4,512]{2,1,0:T(4,128)(2,1)} fusion(bf16[4,768,512]{2,0,1:T(4,128)(2,1)} %constant_dynamic-update-slice_fusion.5, s32[8192]{0:T(1024)S(1)} %broadcast_clamp_fusion), kind=kCustom, calls=%fused_computation.9 | custom fusion | bytes 67141632 | tf_op jit(solution)/shard_map/gather | solution.py:109
  586.4 48.5 %reshape.311 = bf16[4,512,16,4,128]{4,3,0,2,1:T(4,128)(2,1)} reshape(bf16[4,512,16,512]{3,0,2,1:T(4,128)(2,1)} %bitcast.203) | data formatting | bytes 67108864 | tf_op jit(solution)/shard_map/reshape | solution.py:109
  638.1 82.7 %gather_fusion.4 = bf16[8192,4,512]{2,1,0:T(4,128)(2,1)} fusion(bf16[4,768,512]{2,0,1:T(4,128)(2,1)S(1)} %constant_dynamic-update-slice_fusion, s32[8192]{0:T(1024)S(1)} %broadcast_clamp_fusion), kind=kCustom, calls=%fused_computation.4 | custom fusion | bytes 67141632 | tf_op jit(solution)/shard_map/gather | solution.py:108
  720.8 48.5 %reshape.309 = bf16[4,512,16,4,128]{4,3,0,2,1:T(4,128)(2,1)} reshape(bf16[4,512,16,512]{3,0,2,1:T(4,128)(2,1)} %bitcast.202) | data formatting | bytes 67108864 | tf_op jit(solution)/shard_map/reshape | solution.py:108
  769.3 21.9 fusion.13
  791.1 17.7 copy.123
  841.2 27.3 %copy.124 = bf16[4,512,4,16,1]{3,4,2,1,0:T(2,128)(2,1)} copy(bf16[4,512,4,16,1]{2,3,1,0,4:T(8,128)(2,1)} %get-tuple-element.25) | data formatting | bytes 524288 | tf_op jit(solution)/shard_map/convert_element_type | solution.py:119
  868.5 15.0 fusion.9
  896.5 13.7 fusion.17
  949.1 21.9 fusion.7
  971.0 17.6 copy.128
  988.7 34.9 %fusion.68 = (f32[4,512,4,16]{2,3,1,0:T(8,128)}, bf16[4,512,4,16]{2,3,1,0:T(8,128)(2,1)}) fusion(f32[4,512,4,1,16]{2,4,1,0,3:T(8,128)} %copy.128, f32[4,512,4,1,16]{2,4,1,0,3:T(8,128)} %copy.123, f32[4,512,4]{2,1,0:T(8,128)} %copy-done.19), kind=kOutput, calls=%fused_computation.167 | output fusion | flops 1187855 | bytes 1867776 | tf_op jit(solution)/shard_map/sub | solution.py:183
  1023.6 42.7 %multiply_multiply_fusion = f32[4,512,4,128,16]{3,2,4,1,0:T(4,128)} fusion(f32[4,512,4,16]{2,3,1,0:T(8,128)} %get-tuple-element.53, f32[4,512,4,128]{3,2,1,0:T(4,128)S(1)} %copy-done.17), kind=kLoop, calls=%fused_computation.27 | loop fusion | flops 33554432 | bytes 71827456 | tf_op jit(solution)/shard_map/mul | solution.py:191
  1066.3 212.8 %scatter_custom_fusion = f32[3072,512]{1,0:T(8,128)} fusion(s32[32768]{0:T(1024)} %reshape.408, f32[4096,8,4,128]{3,2,1,0:T(4,128)} %bitcast.71, f32[]{:T(128)} %constant.9.clone.1), kind=kCustom, calls=%fused_computation.24 | custom fusion | flops 16777216 | bytes 73400832 | tf_op jit(solution)/shard_map/scatter-add | solution.py:197
  1288.4 27.7 %copy.129 = bf16[4,512,4,16,1]{3,4,2,1,0:T(2,128)(2,1)} copy(bf16[4,512,4,16,1]{2,3,1,0,4:T(8,128)(2,1)} %bitcast.212) | data formatting | bytes 524288 | tf_op jit(solution)/shard_map/convert_element_type | solution.py:184
  1316.1 15.0 fusion.11
  1349.8 42.6 %broadcast_multiply_fusion = f32[4,512,4,128,16]{3,2,4,1,0:T(4,128)} fusion(f32[4,512,4,16]{2,3,1,0:T(8,128)} %get-tuple-element.24, f32[4,512,4,128]{3,2,1,0:T(4,128)S(1)} %copy-done.18), kind=kLoop, calls=%fused_computation.28 | loop fusion | flops 16777216 | bytes 71827456 | tf_op jit(solution)/shard_map/snhk,snhd->snkhd/dot_general | solution.py:179
  1392.4 213.0 %scatter_custom_fusion.5 = f32[3072,512]{1,0:T(8,128)} fusion(s32[32768]{0:T(1024)} %reshape.408, f32[4096,8,4,128]{3,2,1,0:T(4,128)} %bitcast.74, f32[]{:T(128)} %constant.9.clone.1), kind=kCustom, calls=%fused_computation.21 | custom fusion | flops 16777216 | bytes 73400832 | tf_op jit(solution)/shard_map/scatter-add | solution.py:200
  1771.6 37.2 %all-reduce.6 = (f32[2048]{0:T(1024)S(1)}, f32[512]{0:T(512)S(1)}, f32[2048]{0:T(1024)S(1)}) all-reduce(f32[2048]{0:T(1024)S(1)} %copy-done.65, f32[512]{0:T(512)S(1)} %get-tuple-element.36, f32[2048]{0:T(1024)S(1)} %fusion.53), channel_id=7, replica_groups=mesh['patch'=16,'sample'=2] {'patch','sample'}, use_global_device_ids=true, to_apply=%region_27.0.clone | all-reduce | flops 4608 | bytes 36864
  1810.5 32.9 %reduce-scatter.22.cloned.1.call-done = f32[64,16]{1,0:T(8,128)} async-done(((f32[2048,16]{1,0:T(8,128)}), f32[64,16]{1,0:T(8,128)}) %reduce-scatter.22.cloned.1.call-update) | async-done | bytes 4112
  1844.9 134.0 %reduce-scatter.16.cloned.1.call-done = f32[16,512]{1,0:T(8,128)} async-done(((f32[512,512]{1,0:T(8,128)}), f32[16,512]{1,0:T(8,128)}) %reduce-scatter.16.cloned.1.call-update) | async-done | bytes 32784 | tf_op jit(solution)/shard_map/reduce_scatter | solution.py:256
  1978.8 135.2 %reduce-scatter.10.cloned.1.call-done = f32[16,512]{1,0:T(8,128)} async-done(((f32[512,512]{1,0:T(8,128)}), f32[16,512]{1,0:T(8,128)}) %reduce-scatter.10.cloned.1.call-update) | async-done | bytes 32784 | tf_op jit(solution)/shard_map/reduce_scatter | solution.py:253
  2114.1 135.2 %reduce-scatter.12.cloned.1.call-done = f32[16,512]{1,0:T(8,128)} async-done(((f32[512,512]{1,0:T(8,128)}), f32[16,512]{1,0:T(8,128)}) %reduce-scatter.12.cloned.1.call-update) | async-done | bytes 32784 | tf_op jit(solution)/shard_map/reduce_scatter | solution.py:254
  2249.3 135.4 %reduce-scatter.14.cloned.1.call-done = f32[16,512]{1,0:T(8,128)} async-done(((f32[512,512]{1,0:T(8,128)}), f32[16,512]{1,0:T(8,128)}) %reduce-scatter.14.cloned.1.call-update) | async-done | bytes 32784 | tf_op jit(solution)/shard_map/reduce_scatter | solution.py:255
  2384.7 142.2 %reduce-scatter.18.cloned.1.call-done = f32[16,2048]{1,0:T(8,128)} async-done(((f32[512,2048]{1,0:T(8,128)}), f32[16,2048]{1,0:T(8,128)}) %reduce-scatter.18.cloned.1.call-update) | async-done | bytes 131088 | tf_op jit(solution)/shard_map/reduce_scatter | solution.py:257
  2526.9 142.8 %reduce-scatter.20.cloned.1.call-done = f32[64,512]{1,0:T(8,128)} async-done(((f32[2048,512]{1,0:T(8,128)}), f32[64,512]{1,0:T(8,128)}) %reduce-scatter.20.cloned.1.call-update) | async-done | bytes 131088 | tf_op jit(solution)/shard_map/reduce_scatter | solution.py:259
  (329 shorter events, 394.1 us)
Async XLA Ops:
  7.2 117.0 %copy-start = (f32[4,16]{1,0:T(4,128)S(1)}, f32[4,16]{1,0:T(4,128)}, u32[]{:S(2)}) copy-start(f32[4,16]{1,0:T(4,128)} %param.18) | copy-start | bytes 772
  7.2 115.9 %copy-start.4 = (bf16[4,512,512]{2,1,0:T(8,128)(2,1)S(1)}, bf16[4,512,512]{2,1,0:T(8,128)(2,1)}, u32[]{:S(2)}) copy-start(bf16[4,512,512]{2,1,0:T(8,128)(2,1)} %param.15) | copy-start | bytes 6291460
  7.2 117.7 %copy-start.52 = (bf16[16,512]{1,0:T(8,128)(2,1)S(1)}, bf16[16,512]{1,0:T(8,128)(2,1)}, u32[]{:S(2)}) copy-start(bf16[16,512]{1,0:T(8,128)(2,1)} %param.20) | copy-start | bytes 49156
  7.2 889.3 %all-gather.4.cloned.1.call-start = ((), (), s32[]{:S(2)}) async-start(), calls=%async_computation.7 | async-start | bytes 2162688 | tf_op jit(solution)/shard_map/all_gather | solution.py:69
  7.9 902.2 %all-gather.6.cloned.1.call-start = ((), (), s32[]{:S(2)}) async-start(), calls=%async_computation.8 | async-start | bytes 2162688 | tf_op jit(solution)/shard_map/all_gather | solution.py:71
  8.8 183.2 %copy-start.60 = (s32[64]{0:T(128)}, s32[64]{0:T(128)S(1)}, u32[]{:S(2)}) copy-start(s32[64]{0:T(128)S(1)} %get-tuple-element.46) | copy-start | bytes 772
  8.8 183.2 %copy-start.62 = (s32[64]{0:T(128)}, s32[64]{0:T(128)S(1)}, u32[]{:S(2)}) copy-start(s32[64]{0:T(128)S(1)} %get-tuple-element.47) | copy-start | bytes 772
  8.8 191.1 %copy-start.56 = (s32[64]{0:T(128)}, s32[64]{0:T(128)S(1)}, u32[]{:S(2)}) copy-start(s32[64]{0:T(128)S(1)} %get-tuple-element.45) | copy-start | bytes 772
  8.9 191.1 %copy-start.58 = (s32[64]{0:T(128)}, s32[64]{0:T(128)S(1)}, u32[]{:S(2)}) copy-start(s32[64]{0:T(128)S(1)} %get-tuple-element.48) | copy-start | bytes 772
  199.9 286.0 %collective-permute-start = (bf16[4,64,512]{2,0,1:T(4,128)(2,1)}, bf16[4,64,512]{2,0,1:T(4,128)(2,1)}, u32[]{:S(2)}, u32[]{:S(2)}) collective-permute-start(bf16[4,64,512]{2,0,1:T(4,128)(2,1)} %bitcast.6), channel_id=1, source_target_pairs={{30,0},{0,2},{2,4},{4,6},{6,8},{8,10},{10,12},{12,14},{14,16},{16,... | collective-permute-start | bytes 786440 | tf_op jit(solution)/shard_map/ppermute | solution.py:16
  203.0 434.0 %collective-permute-start.3 = (bf16[4,64,512]{2,0,1:T(4,128)(2,1)}, bf16[4,64,512]{2,0,1:T(4,128)(2,1)}, u32[]{:S(2)}, u32[]{:S(2)}) collective-permute-start(bf16[4,64,512]{2,0,1:T(4,128)(2,1)} %bitcast.15), channel_id=1, source_target_pairs={{8,0},{10,2},{12,4},{14,6},{16,8},{18,10},{20,12},{22,14},{24,16},... | collective-permute-start | bytes 786440 | tf_op jit(solution)/shard_map/ppermute | solution.py:16
  206.1 428.8 %collective-permute-start.1 = (bf16[4,64,512]{2,0,1:T(4,128)(2,1)}, bf16[4,64,512]{2,0,1:T(4,128)(2,1)}, u32[]{:S(2)}, u32[]{:S(2)}) collective-permute-start(bf16[4,64,512]{2,0,1:T(4,128)(2,1)} %bitcast.9), channel_id=1, source_target_pairs={{2,0},{4,2},{6,4},{8,6},{10,8},{12,10},{14,12},{16,14},{18,16},{20... | collective-permute-start | bytes 786440 | tf_op jit(solution)/shard_map/ppermute | solution.py:16
  289.6 197.5 %collective-permute-start.4 = (bf16[4,64,512]{2,0,1:T(4,128)(2,1)}, bf16[4,64,512]{2,0,1:T(4,128)(2,1)}, u32[]{:S(2)}, u32[]{:S(2)}) collective-permute-start(bf16[4,64,512]{2,0,1:T(4,128)(2,1)} %bitcast.21), channel_id=1, source_target_pairs={{30,0},{0,2},{2,4},{4,6},{6,8},{8,10},{10,12},{12,14},{14,16},{16,... | collective-permute-start | bytes 786440 | tf_op jit(solution)/shard_map/ppermute | solution.py:16
  303.8 188.9 %collective-permute-start.5 = (bf16[4,64,512]{2,0,1:T(4,128)(2,1)}, bf16[4,64,512]{2,0,1:T(4,128)(2,1)}, u32[]{:S(2)}, u32[]{:S(2)}) collective-permute-start(bf16[4,64,512]{2,0,1:T(4,128)(2,1)} %bitcast.22), channel_id=1, source_target_pairs={{2,0},{4,2},{6,4},{8,6},{10,8},{12,10},{14,12},{16,14},{18,16},{20... | collective-permute-start | bytes 786440 | tf_op jit(solution)/shard_map/ppermute | solution.py:16
  308.3 1535.2 %reduce-scatter.22.cloned.1.call-start = ((), (), s32[]{:S(2)}) async-start(), calls=%async_computation.15 | async-start | bytes 1081344
  486.0 11.1 collective-permute-start.6
  487.1 14.1 collective-permute-start.7
  492.7 143.3 %collective-permute-start.2 = (bf16[4,64,512]{2,0,1:T(4,128)(2,1)S(1)}, bf16[4,64,512]{2,0,1:T(4,128)(2,1)}, u32[]{:S(2)}, u32[]{:S(2)}) collective-permute-start(bf16[4,64,512]{2,0,1:T(4,128)(2,1)S(1)} %bitcast.233), channel_id=1, source_target_pairs={{24,0},{26,2},{28,4},{30,6},{0,8},{2,10},{4,12},{6,14},{8,16},{10,... | collective-permute-start | bytes 786440 | tf_op jit(solution)/shard_map/ppermute | solution.py:16
  1341.5 274.0 %collective-permute-start.11 = (bf16[4,64,512]{2,1,0:T(8,128)(2,1)}, bf16[4,64,512]{2,1,0:T(8,128)(2,1)S(1)}, u32[]{:S(2)}, u32[]{:S(2)}) collective-permute-start(bf16[4,64,512]{2,1,0:T(8,128)(2,1)} %get-tuple-element.32), channel_id=1, source_target_pairs={{24,0},{26,2},{28,4},{30,6},{0,8},{2,10},{4,12},{6,14},{8,16},{10,... | collective-permute-start | bytes 786440 | tf_op jit(solution)/shard_map/ppermute | solution.py:16
  1341.5 277.9 %collective-permute-start.10 = (bf16[4,64,512]{2,1,0:T(8,128)(2,1)}, bf16[4,64,512]{2,1,0:T(8,128)(2,1)S(1)}, u32[]{:S(2)}, u32[]{:S(2)}) collective-permute-start(bf16[4,64,512]{2,1,0:T(8,128)(2,1)} %get-tuple-element.33), channel_id=1, source_target_pairs={{8,0},{10,2},{12,4},{14,6},{16,8},{18,10},{20,12},{22,14},{24,16},... | collective-permute-start | bytes 786440 | tf_op jit(solution)/shard_map/ppermute | solution.py:16
  1345.4 274.2 %collective-permute-start.9 = (bf16[4,64,512]{2,1,0:T(8,128)(2,1)S(1)}, bf16[4,64,512]{2,1,0:T(8,128)(2,1)S(1)}, u32[]{:S(2)}, u32[]{:S(2)}) collective-permute-start(bf16[4,64,512]{2,1,0:T(8,128)(2,1)S(1)} %get-tuple-element.34), channel_id=1, source_target_pairs={{30,0},{0,2},{2,4},{4,6},{6,8},{8,10},{10,12},{12,14},{14,16},{16,... | collective-permute-start | bytes 786440 | tf_op jit(solution)/shard_map/ppermute | solution.py:16
  1345.4 278.8 %collective-permute-start.8 = (bf16[4,64,512]{2,1,0:T(8,128)(2,1)}, bf16[4,64,512]{2,1,0:T(8,128)(2,1)S(1)}, u32[]{:S(2)}, u32[]{:S(2)}) collective-permute-start(bf16[4,64,512]{2,1,0:T(8,128)(2,1)} %get-tuple-element.35), channel_id=1, source_target_pairs={{2,0},{4,2},{6,4},{8,6},{10,8},{12,10},{14,12},{16,14},{18,16},{20... | collective-permute-start | bytes 786440 | tf_op jit(solution)/shard_map/ppermute | solution.py:16
  1615.5 9.0 collective-permute-start.15
  1615.6 46.1 %collective-permute-start.14 = (bf16[4,64,512]{2,1,0:T(8,128)(2,1)}, bf16[4,64,512]{2,1,0:T(8,128)(2,1)S(1)}, u32[]{:S(2)}, u32[]{:S(2)}) collective-permute-start(bf16[4,64,512]{2,1,0:T(8,128)(2,1)} %get-tuple-element.29), channel_id=1, source_target_pairs={{8,0},{10,2},{12,4},{14,6},{16,8},{18,10},{20,12},{22,14},{24,16},... | collective-permute-start | bytes 786440 | tf_op jit(solution)/shard_map/ppermute | solution.py:16
  1619.4 42.6 %collective-permute-start.13 = (bf16[4,64,512]{2,1,0:T(8,128)(2,1)}, bf16[4,64,512]{2,1,0:T(8,128)(2,1)S(1)}, u32[]{:S(2)}, u32[]{:S(2)}) collective-permute-start(bf16[4,64,512]{2,1,0:T(8,128)(2,1)} %get-tuple-element.30), channel_id=1, source_target_pairs={{30,0},{0,2},{2,4},{4,6},{6,8},{8,10},{10,12},{12,14},{14,16},{16,... | collective-permute-start | bytes 786440 | tf_op jit(solution)/shard_map/ppermute | solution.py:16
  1619.6 46.1 %collective-permute-start.12 = (bf16[4,64,512]{2,1,0:T(8,128)(2,1)}, bf16[4,64,512]{2,1,0:T(8,128)(2,1)S(1)}, u32[]{:S(2)}, u32[]{:S(2)}) collective-permute-start(bf16[4,64,512]{2,1,0:T(8,128)(2,1)} %get-tuple-element.31), channel_id=1, source_target_pairs={{2,0},{4,2},{6,4},{8,6},{10,8},{12,10},{14,12},{16,14},{18,16},{20... | collective-permute-start | bytes 786440 | tf_op jit(solution)/shard_map/ppermute | solution.py:16
  1708.9 269.9 %reduce-scatter.16.cloned.1.call-start = ((), (), s32[]{:S(2)}) async-start(), calls=%async_computation.12 | async-start | bytes 1081344 | tf_op jit(solution)/shard_map/reduce_scatter | solution.py:256
  1713.5 400.6 %reduce-scatter.10.cloned.1.call-start = ((), (), s32[]{:S(2)}) async-start(), calls=%async_computation.9 | async-start | bytes 1081344 | tf_op jit(solution)/shard_map/reduce_scatter | solution.py:253
  1718.1 531.3 %reduce-scatter.12.cloned.1.call-start = ((), (), s32[]{:S(2)}) async-start(), calls=%async_computation.10 | async-start | bytes 1081344 | tf_op jit(solution)/shard_map/reduce_scatter | solution.py:254
  1722.7 662.0 %reduce-scatter.14.cloned.1.call-start = ((), (), s32[]{:S(2)}) async-start(), calls=%async_computation.11 | async-start | bytes 1081344 | tf_op jit(solution)/shard_map/reduce_scatter | solution.py:255
  1727.3 799.6 %reduce-scatter.18.cloned.1.call-start = ((), (), s32[]{:S(2)}) async-start(), calls=%async_computation.13 | async-start | bytes 4325376 | tf_op jit(solution)/shard_map/reduce_scatter | solution.py:257
  1738.0 931.7 %reduce-scatter.20.cloned.1.call-start = ((), (), s32[]{:S(2)}) async-start(), calls=%async_computation.14 | async-start | bytes 4325376 | tf_op jit(solution)/shard_map/reduce_scatter | solution.py:259
  (64 other events, 894.3 us)
Sparse Core Ops, SparseCore 0:
  11.1 59.2 all-gather.3
  308.4 52.3 all-gather.5
  1709.0 134.3 reduce-scatter.21
  1846.1 132.6 reduce-scatter.15
  1981.5 132.5 reduce-scatter.9
  2116.7 132.5 reduce-scatter.11
  2252.1 132.5 reduce-scatter.13
  2387.6 139.3 reduce-scatter.17
  2529.8 139.9 reduce-scatter.19
where the time goes:
time: 2690 us; the launch traced here: 2680 us
  waiting for transfers between devices  865 us (32%)
  other arithmetic  696 us (26%)
  local copies, waits for them, and re-layouts  460 us (17%)
  blocking collectives  421 us (16%)
  matrix products  178 us (7%)
  starting transfers between devices  41 us (2%)
    scatter-add x1, other arithmetic, body(): jax.ops.segment_sum(grad_value_near.reshape(-1, width), slots, num_segmen...  213 us
    scatter-add x1, other arithmetic, body(): jax.ops.segment_sum(grad_key_near.reshape(-1, width), slots, num_segments...  213 us
    reduce_scatter x1, waiting for transfers between devices, body(): lax.psum_scatter(grad_down, ('patch', 'sample'), scatter_dimension=0, til...  143 us
    reduce_scatter x1, waiting for transfers between devices, body(): lax.psum_scatter(grad_up, ('patch', 'sample'), scatter_dimension=0, tiled...  142 us
    reduce_scatter x1, waiting for transfers between devices, body(): lax.psum_scatter(grad_value, ('patch', 'sample'), scatter_dimension=0, ti...  135 us
    reduce_scatter x1, waiting for transfers between devices, body(): lax.psum_scatter(grad_key, ('patch', 'sample'), scatter_dimension=0, tile...  135 us
    reduce_scatter x1, waiting for transfers between devices, body(): lax.psum_scatter(grad_query, ('patch', 'sample'), scatter_dimension=0, ti...  135 us
    reduce_scatter x1, waiting for transfers between devices, body(): lax.psum_scatter(grad_out_proj, ('patch', 'sample'), scatter_dimension=0,...  134 us
  transfers between devices with their start and end apart: 25, of which 10 were waited for; matrix products, arithmetic and copies ran while one was open for 32% of the time, Pallas kernels for 0%

commit v1 on v0

v1 whole, which is shorter than its diff:
```python
import math

import jax
import jax.numpy as jnp
from jax import lax
from jax.experimental import pallas as pl
from jax.experimental.pallas import tpu as pltpu
from jax.sharding import PartitionSpec as P

HEAD = 128
STRIDE = 4
BLOCK = 16
AXES = ("patch", "sample")
EPSILON = 1e-05
F32 = jnp.float32
BF16 = jnp.bfloat16
VMEM_LIMIT = 60 * 1024 * 1024


def product(left, right):
    return jnp.dot(left, right, preferred_element_type=F32)


def product_t(left, right):
    return lax.dot_general(left, right, (((1,), (1,)), ((), ())), preferred_element_type=F32)


def from_behind(block, distance):
    count = lax.axis_size("patch")
    return lax.ppermute(block, "patch", [((i - distance) % count, i) for i in range(count)])


def swap(block, bits, devices):
    return lax.ppermute(block, AXES, [(i, i ^ bits) for i in range(devices)])


def stage_groups(devices):
    bits = [1 << i for i in reversed(range(devices.bit_length() - 1)) if (1 << i) != 2]
    groups = [bits[i : i + 2] for i in range(0, len(bits), 2)]
    return [combos(g) for g in groups] + [[2]]


def combos(group):
    if len(group) == 1:
        return [group[0]]
    high, low = group
    return [low, high, low | high]


def relative(k, devices):
    shift, out = 0, 0
    for group in stage_groups(devices):
        if len(group) == 1:
            out = out | (((k >> shift) & 1) * group[0])
            shift += 1
        else:
            out = out | (((k >> shift) & 1) * group[0]) | (((k >> (shift + 1)) & 1) * group[1])
            shift += 2
    return out


def gather_shards(shard, devices):
    groups = stage_groups(devices)
    held = shard[None]
    for group in groups[:-1]:
        held = jnp.concatenate([held] + [swap(held, c, devices) for c in group], axis=0)
    return held, swap(held, groups[-1][0], devices)


def scatter_shards(low_half, high_half, devices):
    groups = stage_groups(devices)
    got = swap(high_half, groups[-1][0], devices)
    held = (low_half.astype(F32) + got.astype(F32)).astype(BF16)
    for at, group in reversed(list(enumerate(groups[:-1]))):
        parts = len(group) + 1
        size = held.shape[0] // parts
        total = held[:size].astype(F32)
        pieces = [
            swap(held[(i + 1) * size : (i + 2) * size], c, devices) for i, c in enumerate(group)
        ]
        for piece in pieces:
            total = total + piece.astype(F32)
        held = total if at == 0 else total.astype(BF16)
    return held[0]


def layer_normalize(values):
    centre = jnp.mean(values, axis=-1, keepdims=True)
    centred = values - centre
    inverse = lax.rsqrt(jnp.mean(centred * centred, axis=-1, keepdims=True) + EPSILON)
    return centred * inverse, inverse


def norm_back(grad_hat, normed, inverse):
    first = jnp.mean(grad_hat, axis=-1, keepdims=True)
    second = jnp.mean(grad_hat * normed, axis=-1, keepdims=True)
    return inverse * (grad_hat - first - normed * second)


def whole(shape):
    return pl.BlockSpec(shape, lambda *_: (0,) * len(shape))


def per_sample(shape):
    return pl.BlockSpec((1,) + shape, lambda s, *_: (s,) + (0,) * len(shape))


def params():
    return pltpu.CompilerParams(
        dimension_semantics=("arbitrary",), vmem_limit_bytes=VMEM_LIMIT
    )


def prepare_kernel(nodes_ref, send_ref, nbr_ref, bias_ref, *out_refs):
    samples, count, _ = nodes_ref.shape
    picks = send_ref.shape[0]
    table = bias_ref.shape[0]
    near = nbr_ref.shape[0]
    place = lax.broadcasted_iota(jnp.int32, (table, count), 0)
    total = jnp.zeros((table, count), F32)
    for j in range(near):
        total = total + jnp.where(place == nbr_ref[j : j + 1, :], 1.0, 0.0)
    bias_ref[...] = jnp.where(total > 0.0, jnp.log2(jnp.maximum(total, 1.0)), -1e30)
    lanes = lax.broadcasted_iota(jnp.int32, (picks, count), 1)
    chosen = jnp.where(lanes == send_ref[...], 1.0, 0.0).astype(BF16)
    each = picks // len(out_refs)
    for s in range(samples):
        rows = product(chosen, nodes_ref[s]).astype(BF16)
        for d, out_ref in enumerate(out_refs):
            out_ref[s] = rows[d * each : (d + 1) * each]


def prepare(nodes, neighbours, send_rows):
    samples, count, width = nodes.shape
    ways, each = send_rows.shape
    table = count + ways * each
    send_column = send_rows.reshape(ways * each, 1)
    out = [jax.ShapeDtypeStruct((table, count), F32)] + [
        jax.ShapeDtypeStruct((samples, each, width), BF16)
    ] * ways
    return pl.pallas_call(
        prepare_kernel,
        out_shape=out,
        compiler_params=pltpu.CompilerParams(vmem_limit_bytes=VMEM_LIMIT),
    )(nodes, send_column, neighbours.T)


def spread(rows, step, width):
    reps = jnp.concatenate([rows] * (width // 128), axis=1)
    lane = lax.broadcasted_iota(jnp.int32, reps.shape, 1)
    row = lax.broadcasted_iota(jnp.int32, reps.shape, 0)
    return jnp.sum(jnp.where(lane // step == row, reps, 0.0), axis=0, keepdims=True)


def first_weights_kernel(me_ref, low_ref, high_ref, code_ref, wq_ref, wk_ref, wv_ref, mod_ref, raw):
    half = low_ref.shape[0]
    devices = 2 * half
    samples = code_ref.shape[1]
    width = wq_ref.shape[1]
    step = 4 * width // devices
    code = code_ref[...]
    for k in range(devices):
        source = low_ref if k < half else high_ref
        shard = me_ref[0] ^ relative(k, devices)
        rows = pl.ds(pl.multiple_of(shard * BLOCK, BLOCK), BLOCK)
        wq_ref[rows, :] = source[k % half, 0:BLOCK, :]
        wk_ref[rows, :] = source[k % half, BLOCK : 2 * BLOCK, :]
        wv_ref[rows, :] = source[k % half, 2 * BLOCK : 3 * BLOCK, :]
        cond = source[k % half, 3 * BLOCK : 4 * BLOCK, 0:128].astype(F32)
        bias = source[k % half, 3 * BLOCK : 4 * BLOCK, 128:256].astype(F32)[0:1]
        for s in range(samples):
            value = jnp.sum(cond * code[:, s : s + 1], axis=0, keepdims=True) + bias
            raw[s, pl.ds(shard, 1), :] = value
    each = devices // 4
    for s in range(samples):
        for kind in range(4):
            value = spread(raw[s, kind * each : (kind + 1) * each, :], step, width)
            mod_ref[s, kind : kind + 1, :] = value + 1.0 if kind % 2 == 0 else value


def second_weights_kernel(me_ref, low_ref, high_ref, wo_ref, wu_ref, wd_ref, bu_ref, bd_ref, raw):
    half = low_ref.shape[0]
    devices = 2 * half
    width = wo_ref.shape[1]
    hidden = wu_ref.shape[1]
    wide = hidden // width
    down = hidden // devices
    for k in range(devices):
        source = low_ref if k < half else high_ref
        shard = me_ref[0] ^ relative(k, devices)
        rows = pl.ds(pl.multiple_of(shard * BLOCK, BLOCK), BLOCK)
        long_rows = pl.ds(pl.multiple_of(shard * down, BLOCK), down)
        at = 0
        for c in range(wide):
            wu_ref[rows, c * width : (c + 1) * width] = source[k % half, at : at + BLOCK, :]
            at += BLOCK
        wd_ref[long_rows, :] = source[k % half, at : at + down, :]
        at += down
        wo_ref[rows, :] = source[k % half, at : at + BLOCK, :]
        at += BLOCK
        extra = source[k % half, at : at + BLOCK, 0:256].astype(F32)[0:1]
        raw[0, pl.ds(shard, 1), :] = extra[:, 0:128]
        raw[1, pl.ds(shard, 1), :] = extra[:, 128:256]
    each = devices // wide
    for c in range(wide):
        bu_ref[:, c * width : (c + 1) * width] = spread(
            raw[0, c * each : (c + 1) * each, :], hidden // devices, width
        )
    bd_ref[...] = spread(raw[1], width // devices, width)


def packs(width, devices):
    return width == devices * BLOCK


def gather_plain(wq, wk, wv, cond_weight, cond_bias, noise_code, wo, wu, bu, wd, bd):
    def full(x, axis=0):
        return lax.all_gather(x, AXES, axis=axis, tiled=True)

    mod = jnp.dot(
        noise_code, full(cond_weight, 1).astype(F32), precision=lax.Precision.HIGHEST
    ) + full(cond_bias).astype(F32)
    mod = mod.reshape(noise_code.shape[0], 4, wq.shape[1])
    mod = mod + jnp.array([1.0, 0.0, 1.0, 0.0], F32)[:, None]
    first = (full(wq), full(wk), full(wv), mod)
    biases = (full(bu)[None].astype(F32), full(bd)[None].astype(F32))
    return first, (full(wo), full(wu), full(wd)) + biases


def scatter_plain(sums, axes):
    return [
        lax.psum_scatter(x, AXES, scatter_dimension=axis, tiled=True)
        for x, axis in zip(sums, axes)
    ]


def repeat_lanes(rows, lanes=128):
    return jnp.tile(rows, (1, lanes // rows.shape[1]))


def fit(rows, height, width):
    return jnp.pad(rows, ((0, height - rows.shape[0]), (0, width - rows.shape[1])))


def smem():
    return pl.BlockSpec(memory_space=pltpu.SMEM)


def gather_first(me, wq, wk, wv, cond_weight, cond_bias, noise_code, devices):
    width = wq.shape[1]
    extra = jnp.concatenate(
        [repeat_lanes(cond_weight), fit(repeat_lanes(cond_bias[None]), BLOCK, 128)], axis=1
    )
    shard = jnp.concatenate([wq, wk, wv, fit(extra, BLOCK, width)], axis=0)
    low_half, high_half = gather_shards(shard, devices)
    samples = noise_code.shape[0]
    full = jax.ShapeDtypeStruct((width, width), BF16)
    return pl.pallas_call(
        first_weights_kernel,
        out_shape=[full, full, full, jax.ShapeDtypeStruct((samples, 4, width), F32)],
        in_specs=[smem()] + [pl.BlockSpec(memory_space=pltpu.VMEM)] * 3,
        scratch_shapes=[pltpu.VMEM((samples, devices, 128), F32)],
        compiler_params=pltpu.CompilerParams(vmem_limit_bytes=VMEM_LIMIT),
    )(me, low_half, high_half, noise_code.T)


def gather_second(me, wo, wu, bu, wd, bd, devices):
    width = wo.shape[1]
    hidden = wu.shape[1]
    extra = jnp.concatenate([repeat_lanes(bu[None]), repeat_lanes(bd[None])], axis=1)
    parts = [wu[:, c * width : (c + 1) * width] for c in range(hidden // width)]
    shard = jnp.concatenate(parts + [wd, wo, fit(extra, BLOCK, width)], axis=0)
    low_half, high_half = gather_shards(shard, devices)
    return pl.pallas_call(
        second_weights_kernel,
        out_shape=[
            jax.ShapeDtypeStruct((width, width), BF16),
            jax.ShapeDtypeStruct((width, hidden), BF16),
            jax.ShapeDtypeStruct((hidden, width), BF16),
            jax.ShapeDtypeStruct((1, hidden), F32),
            jax.ShapeDtypeStruct((1, width), F32),
        ],
        in_specs=[smem()] + [pl.BlockSpec(memory_space=pltpu.VMEM)] * 2,
        scratch_shapes=[pltpu.VMEM((2, devices, 128), F32)],
        compiler_params=pltpu.CompilerParams(vmem_limit_bytes=VMEM_LIMIT),
    )(me, low_half, high_half)


def attend_kernel(*refs):
    nodes_ref, h0, h1, h2, h3, mod_ref, wq_ref, wk_ref, wv_ref, bias_ref = refs[:10]
    act_ref, q_ref, k_ref, v_ref, p_ref, att_ref = refs[10:]
    count = nodes_ref.shape[1]
    each = h0.shape[1]
    width = nodes_ref.shape[2]
    scale, shift = mod_ref[0, 0:1, :], mod_ref[0, 1:2, :]

    def activate(rows):
        hat, _ = layer_normalize(rows.astype(F32))
        return (hat * scale + shift).astype(BF16)

    act_ref[0, 0:count, :] = activate(nodes_ref[0])
    for d, ref in enumerate((h0, h1, h2, h3)):
        at = count + d * each
        act_ref[0, at : at + each, :] = activate(ref[0])
    act = act_ref[0]
    q_ref[0] = product(act[0:count], wq_ref[...]).astype(BF16)
    k_ref[0] = product(act, wk_ref[...]).astype(BF16)
    v_ref[0] = product(act, wv_ref[...]).astype(BF16)
    factor = math.log2(math.e) * HEAD ** (-0.5)
    for h in range(width // HEAD):
        cols = slice(h * HEAD, (h + 1) * HEAD)
        scores = product_t(k_ref[0, :, cols], q_ref[0, :, cols]) * factor + bias_ref[...]
        top = jnp.max(scores, axis=0, keepdims=True)
        expo = jnp.exp2(scores - top)
        total = jnp.sum(expo, axis=0, keepdims=True)
        probs = (expo * (1.0 / total)).astype(BF16)
        p_ref[0, h] = probs
        mixed = product(v_ref[0, :, cols].T, probs)
        att_ref[0, :, cols] = mixed.T.astype(BF16)


def attend(nodes, halos, mod, wq, wk, wv, bias):
    samples, count, width = nodes.shape
    table = bias.shape[0]
    heads = width // HEAD
    each = halos[0].shape[1]

    def out(rows):
        return jax.ShapeDtypeStruct((samples, rows, width), BF16)

    return pl.pallas_call(
        attend_kernel,
        grid=(samples,),
        in_specs=[per_sample((count, width))]
        + [per_sample((each, width))] * 4
        + [per_sample((4, width))]
        + [whole((width, width))] * 3
        + [whole((table, count))],
        out_specs=[per_sample((table, width)), per_sample((count, width))]
        + [per_sample((table, width))] * 2
        + [per_sample((heads, table, count)), per_sample((count, width))],
        out_shape=[out(table), out(count), out(table), out(table)]
        + [jax.ShapeDtypeStruct((samples, heads, table, count), BF16), out(count)],
        compiler_params=params(),
    )(nodes, *halos, mod, wq, wk, wv, bias)


def feed_kernel(*refs):
    me_ref, nodes_ref, att_ref, cot_ref, mod_ref, wo_ref, wu_ref, wd_ref, bu_ref, bd_ref = refs[:10]
    out_ref, gmid_ref, gatt_ref, gmod_ref = refs[10:14]
    sums = refs[14:-6]
    up_acc, down_acc, wo_acc, bu_acc, bd_acc, down_rows = refs[-6:]
    s = pl.program_id(0)
    count, width = nodes_ref.shape[1:]
    hidden_size = wu_ref.shape[1]
    wide = hidden_size // width

    @pl.when(s == 0)
    def _():
        up_acc[...] = jnp.zeros_like(up_acc)
        down_acc[...] = jnp.zeros_like(down_acc)
        wo_acc[...] = jnp.zeros_like(wo_acc)
        bu_acc[...] = jnp.zeros_like(bu_acc)
        bd_acc[...] = jnp.zeros_like(bd_acc)

    scale, shift = mod_ref[0, 2:3, :], mod_ref[0, 3:4, :]
    attended = att_ref[0]
    cot = cot_ref[0]
    cot_float = cot.astype(F32)
    middle = nodes_ref[0].astype(F32) + product(attended, wo_ref[...])
    hat, inverse = layer_normalize(middle)
    act = (hat * scale + shift).astype(BF16)
    act_t = act.T
    cot_t = cot.T
    result = middle + bd_ref[...]
    grad_act = jnp.zeros((count, width), F32)
    bd_acc[...] += jnp.sum(cot_float, axis=0, keepdims=True)
    for c in range(wide):
        cols = slice(c * width, (c + 1) * width)
        w_up = wu_ref[:, cols]
        w_down = wd_ref[cols, :]
        pre = product(act, w_up) + bu_ref[:, cols]
        gate = 0.5 * jnp.tanh(0.5 * pre) + 0.5
        value = pre * gate
        hidden = value.astype(BF16)
        result = result + product(hidden, w_down)
        down_acc[:, cols] += product(cot_t, hidden)
        grad_pre = product_t(cot, w_down) * (gate + value * (1.0 - gate))
        low_pre = grad_pre.astype(BF16)
        bu_acc[:, cols] += jnp.sum(low_pre.astype(F32), axis=0, keepdims=True)
        up_acc[:, cols] += product(act_t, low_pre)
        grad_act = grad_act + product_t(low_pre, w_up)
    out_ref[0] = result.astype(BF16)
    gmod_ref[0, 0:1, :] = jnp.sum(grad_act * hat, axis=0, keepdims=True)
    gmod_ref[0, 1:2, :] = jnp.sum(grad_act, axis=0, keepdims=True)
    grad_middle = cot_float + norm_back(grad_act * scale, hat, inverse)
    gmid_ref[0] = grad_middle
    branch = grad_middle.astype(BF16)
    wo_acc[...] += product(attended.T, branch)
    gatt_ref[0] = product_t(branch, wo_ref[...]).astype(BF16)

    @pl.when(s == pl.num_programs(0) - 1)
    def _():
        for c in range(wide):
            cols = slice(c * width, (c + 1) * width)
            down_rows[cols, :] = down_acc[:, cols].T
        if len(sums) > 2:
            for ref, value in zip(sums, (up_acc, down_rows, wo_acc, bu_acc, bd_acc)):
                ref[...] = value[...]
            return
        low_ref, high_ref = sums
        half = low_ref.shape[0]
        devices = 2 * half
        down = hidden_size // devices

        for part, ref in enumerate((low_ref, high_ref)):

            def pack(i, _, part=part, ref=ref):
                shard = me_ref[0] ^ relative(i + part * half, devices)
                rows = pl.ds(pl.multiple_of(shard * BLOCK, BLOCK), BLOCK)
                long_rows = pl.ds(pl.multiple_of(shard * down, BLOCK), down)
                at = 0
                for c in range(wide):
                    ref[i, at : at + BLOCK, :] = up_acc[rows, c * width : (c + 1) * width].astype(
                        BF16
                    )
                    at += BLOCK
                ref[i, at : at + down, :] = down_rows[long_rows, :].astype(BF16)
                at += down
                ref[i, at : at + BLOCK, :] = wo_acc[rows, :].astype(BF16)
                at += BLOCK
                up_tile = pl.multiple_of(((shard * (hidden_size // devices)) // 128) * 128, 128)
                down_tile = pl.multiple_of(((shard * (width // devices)) // 128) * 128, 128)
                ref[i, at : at + BLOCK, 0:128] = jnp.broadcast_to(
                    bu_acc[:, pl.ds(up_tile, 128)], (BLOCK, 128)
                ).astype(BF16)
                ref[i, at : at + BLOCK, 128:256] = jnp.broadcast_to(
                    bd_acc[:, pl.ds(down_tile, 128)], (BLOCK, 128)
                ).astype(BF16)
                ref[i, at : at + BLOCK, 256:] = jnp.zeros((BLOCK, width - 256), BF16)
                return 0

            lax.fori_loop(0, half, pack, 0)


def feed(me, nodes, attended, cot, mod, wo, wu, wd, bu, bd, devices):
    samples, count, width = nodes.shape
    hidden = wu.shape[1]
    rows = hidden // width * BLOCK + hidden // devices + 2 * BLOCK
    half = devices // 2
    tile = per_sample((count, width))
    packed = (half, rows, width)
    sums = [jax.ShapeDtypeStruct(packed, BF16)] * 2
    if not packs(width, devices):
        plain = ((width, hidden), (hidden, width), (width, width), (1, hidden), (1, width))
        sums = [jax.ShapeDtypeStruct(shape, F32) for shape in plain]
    return pl.pallas_call(
        feed_kernel,
        grid=(samples,),
        in_specs=[smem(), tile, tile, tile, per_sample((4, width))]
        + [whole((width, width)), whole((width, hidden)), whole((hidden, width))]
        + [whole((1, hidden)), whole((1, width))],
        out_specs=[tile, tile, tile, per_sample((2, width))] + [whole(x.shape) for x in sums],
        out_shape=[
            jax.ShapeDtypeStruct((samples, count, width), BF16),
            jax.ShapeDtypeStruct((samples, count, width), F32),
            jax.ShapeDtypeStruct((samples, count, width), BF16),
            jax.ShapeDtypeStruct((samples, 2, width), F32),
        ]
        + sums,
        scratch_shapes=[
            pltpu.VMEM((width, hidden), F32),
            pltpu.VMEM((width, hidden), F32),
            pltpu.VMEM((width, width), F32),
            pltpu.VMEM((1, hidden), F32),
            pltpu.VMEM((1, width), F32),
            pltpu.VMEM((hidden, width), F32),
        ],
        compiler_params=params(),
    )(me, nodes, attended, cot, mod, wo, wu, wd, bu, bd)


def attend_back_kernel(*refs):
    me_ref, nodes_ref, h0, h1, h2, h3, code_ref, gmod_ref = refs[:8]
    act_ref, q_ref, k_ref, v_ref, p_ref, gatt_ref, wq_ref, wk_ref, wv_ref = refs[8:17]
    gact_ref, b0, b1, b2, b3 = refs[17:22]
    outs = refs[22:-8]
    gq, gk, gv, q_acc, k_acc, v_acc, cond_acc, bias_acc = refs[-8:]
    s = pl.program_id(0)
    count, width = nodes_ref.shape[1:]
    each = h0.shape[1]
    inv_root = HEAD ** (-0.5)

    @pl.when(s == 0)
    def _():
        q_acc[...] = jnp.zeros_like(q_acc)
        k_acc[...] = jnp.zeros_like(k_acc)
        v_acc[...] = jnp.zeros_like(v_acc)
        cond_acc[...] = jnp.zeros_like(cond_acc)
        bias_acc[...] = jnp.zeros_like(bias_acc)

    for h in range(width // HEAD):
        cols = slice(h * HEAD, (h + 1) * HEAD)
        probs = p_ref[0, h]
        grad_att = gatt_ref[0, :, cols]
        keys = k_ref[0, :, cols]
        probs_float = probs.astype(F32)
        grad_probs = product_t(v_ref[0, :, cols], grad_att)
        inner = jnp.sum(probs_float * grad_probs, axis=0, keepdims=True)
        grad_scores = (probs_float * (grad_probs - inner)).astype(BF16)
        gv[:, cols] = product(probs, grad_att).astype(BF16)
        gk[:, cols] = (product(grad_scores, q_ref[0, :, cols]) * inv_root).astype(BF16)
        gq[:, cols] = (product(keys.T, grad_scores) * inv_root).T.astype(BF16)

    act_t = act_ref[0].T
    q_acc[...] += product(act_t[:, 0:count], gq[...])
    k_acc[...] += product(act_t, gk[...])
    v_acc[...] += product(act_t, gv[...])
    grad_act = (
        product_t(gq[...], wq_ref[...])
        + product_t(gk[0:count, :], wk_ref[...])
        + product_t(gv[0:count, :], wv_ref[...])
    )
    gact_ref[0] = grad_act
    grad_far = product_t(gk[count:, :], wk_ref[...]) + product_t(gv[count:, :], wv_ref[...])
    hat, _ = layer_normalize(nodes_ref[0].astype(F32))
    scale_sum = jnp.sum(grad_act * hat, axis=0, keepdims=True)
    shift_sum = jnp.sum(grad_act, axis=0, keepdims=True)
    for d, (far, back) in enumerate(zip((h0, h1, h2, h3), (b0, b1, b2, b3))):
        part = grad_far[d * each : (d + 1) * each]
        far_hat, _ = layer_normalize(far[0].astype(F32))
        scale_sum = scale_sum + jnp.sum(part * far_hat, axis=0, keepdims=True)
        shift_sum = shift_sum + jnp.sum(part, axis=0, keepdims=True)
        back[0] = part.astype(BF16)
    sums = (scale_sum, shift_sum, gmod_ref[0, 0:1, :], gmod_ref[0, 1:2, :])
    code = code_ref[0]
    for kind, value in enumerate(sums):
        cols = slice(kind * width, (kind + 1) * width)
        cond_acc[:, cols] += code * value
        bias_acc[:, cols] += value

    @pl.when(s == pl.num_programs(0) - 1)
    def _():
        if len(outs) > 2:
            for ref, value in zip(outs, (q_acc, k_acc, v_acc, cond_acc, bias_acc)):
                ref[...] = value[...]
            return
        half = outs[0].shape[0]
        devices = 2 * half
        for part, ref in enumerate(outs):

            def pack(i, _, part=part, ref=ref):
                shard = me_ref[0] ^ relative(i + part * half, devices)
                rows = pl.ds(pl.multiple_of(shard * BLOCK, BLOCK), BLOCK)
                ref[i, 0:BLOCK, :] = q_acc[rows, :].astype(BF16)
                ref[i, BLOCK : 2 * BLOCK, :] = k_acc[rows, :].astype(BF16)
                ref[i, 2 * BLOCK : 3 * BLOCK, :] = v_acc[rows, :].astype(BF16)
                tile = pl.multiple_of(((shard * (4 * width // devices)) // 128) * 128, 128)
                ref[i, 3 * BLOCK : 4 * BLOCK, 0:128] = cond_acc[:, pl.ds(tile, 128)].astype(BF16)
                ref[i, 3 * BLOCK : 4 * BLOCK, 128:256] = jnp.broadcast_to(
                    bias_acc[:, pl.ds(tile, 128)], (BLOCK, 128)
                ).astype(BF16)
                ref[i, 3 * BLOCK : 4 * BLOCK, 256:] = jnp.zeros((BLOCK, width - 256), BF16)
                return 0

            lax.fori_loop(0, half, pack, 0)


def attend_back(me, nodes, halos, noise_code, gmod, saved, gatt, wq, wk, wv, devices):
    samples, count, width = nodes.shape
    act, queries, keys, values, probs = saved
    table = act.shape[1]
    heads = width // HEAD
    each = halos[0].shape[1]
    half = devices // 2
    codes = noise_code.shape[1]
    code = noise_code[:, :, None]
    sums = [jax.ShapeDtypeStruct((half, 4 * BLOCK, width), BF16)] * 2
    if not packs(width, devices):
        plain = [(width, width)] * 3 + [(codes, 4 * width), (1, 4 * width)]
        sums = [jax.ShapeDtypeStruct(shape, F32) for shape in plain]
    tile, long_tile = per_sample((count, width)), per_sample((table, width))
    small = per_sample((each, width))
    return pl.pallas_call(
        attend_back_kernel,
        grid=(samples,),
        in_specs=[smem(), tile]
        + [small] * 4
        + [per_sample((codes, 1)), per_sample((2, width))]
        + [long_tile, tile, long_tile, long_tile]
        + [per_sample((heads, table, count)), tile]
        + [whole((width, width))] * 3,
        out_specs=[tile] + [small] * 4 + [whole(x.shape) for x in sums],
        out_shape=[jax.ShapeDtypeStruct((samples, count, width), F32)]
        + [jax.ShapeDtypeStruct((samples, each, width), BF16)] * 4
        + sums,
        scratch_shapes=[
            pltpu.VMEM((count, width), BF16),
            pltpu.VMEM((table, width), BF16),
            pltpu.VMEM((table, width), BF16),
            pltpu.VMEM((width, width), F32),
            pltpu.VMEM((width, width), F32),
            pltpu.VMEM((width, width), F32),
            pltpu.VMEM((codes, 4 * width), F32),
            pltpu.VMEM((1, 4 * width), F32),
        ],
        compiler_params=params(),
    )(me, nodes, *halos, code, gmod, act, queries, keys, values, probs, gatt, wq, wk, wv)


def finish_kernel(nodes_ref, gact_ref, b0, b1, b2, b3, send_ref, mod_ref, gmid_ref, out_ref):
    count = nodes_ref.shape[1]
    each = b0.shape[1]
    picks = send_ref.shape[1]
    place = lax.broadcasted_iota(jnp.int32, (count, picks), 0)
    chosen = jnp.where(place == send_ref[...], 1.0, 0.0).astype(BF16)
    grad_act = gact_ref[0]
    for d, ref in enumerate((b0, b1, b2, b3)):
        grad_act = grad_act + product(chosen[:, d * each : (d + 1) * each], ref[0])
    hat, inverse = layer_normalize(nodes_ref[0].astype(F32))
    out_ref[0] = gmid_ref[0] + norm_back(grad_act * mod_ref[0, 0:1, :], hat, inverse)


def finish(nodes, gact, backs, send_rows, mod, gmid):
    samples, count, width = nodes.shape
    each = backs[0].shape[1]
    picks = send_rows.size
    tile = per_sample((count, width))
    return pl.pallas_call(
        finish_kernel,
        grid=(samples,),
        in_specs=[tile, tile]
        + [per_sample((each, width))] * 4
        + [whole((1, picks)), per_sample((4, width)), tile],
        out_specs=tile,
        out_shape=jax.ShapeDtypeStruct((samples, count, width), F32),
        compiler_params=params(),
    )(nodes, gact, *backs, send_rows.reshape(1, picks), mod, gmid)


def own(rows, position, size, axis):
    return lax.dynamic_slice_in_dim(rows, (position * size) % 128, size, axis)


def unpack_feed(total, position, width, hidden, devices):
    wide, down = hidden // width, hidden // devices
    grad_up = jnp.concatenate([total[c * BLOCK : (c + 1) * BLOCK] for c in range(wide)], axis=1)
    at = wide * BLOCK
    last = total[at + down + BLOCK]
    return (
        grad_up,
        total[at : at + down],
        total[at + down : at + down + BLOCK],
        own(last[0:128], position, down, 0),
        own(last[128:256], position, width // devices, 0),
    )


def unpack_proj(total, position, width, devices):
    step = 4 * width // devices
    extra = total[3 * BLOCK : 4 * BLOCK]
    return tuple(total[i * BLOCK : (i + 1) * BLOCK] for i in range(3)) + (
        own(extra[:, 0:128], position, step, 1),
        own(extra[0, 128:256], position, step, 0),
    )


def body(
    nodes,
    neighbours,
    send_rows,
    noise_code,
    w_query,
    w_key,
    w_value,
    w_out,
    w_up,
    b_up,
    w_down,
    b_down,
    cond_weight,
    cond_bias,
    cotangent,
):
    devices = lax.axis_size("patch") * lax.axis_size("sample")
    position = lax.axis_index("patch") * lax.axis_size("sample") + lax.axis_index("sample")
    me = position.astype(jnp.int32).reshape(1)
    width = nodes.shape[2]
    hidden = w_up.shape[1]
    offsets = (1, -1, STRIDE, -STRIDE)

    packed = packs(width, devices)
    bias, *sends = prepare(nodes, neighbours, send_rows)
    if packed:
        first = gather_first(
            me, w_query, w_key, w_value, cond_weight, cond_bias, noise_code, devices
        )
        second = gather_second(me, w_out, w_up, b_up, w_down, b_down, devices)
    else:
        first, second = gather_plain(
            w_query,
            w_key,
            w_value,
            cond_weight,
            cond_bias,
            noise_code,
            w_out,
            w_up,
            b_up,
            w_down,
            b_down,
        )
    wq, wk, wv, mod = first
    halos = [from_behind(block, offset) for block, offset in zip(sends, offsets)]
    *saved, attended = attend(nodes, halos, mod, wq, wk, wv, bias)
    result, gmid, gatt, gmod, *feed_sums = feed(
        me, nodes, attended, cotangent, mod, *second, devices
    )
    if packed:
        feed_sums = unpack_feed(
            scatter_shards(*feed_sums, devices), position, width, hidden, devices
        )
    else:
        feed_sums[3:] = [x[0] for x in feed_sums[3:]]
        feed_sums = scatter_plain(feed_sums, (0,) * 5)
    gact, *rest = attend_back(
        me, nodes, halos, noise_code, gmod, saved, gatt, wq, wk, wv, devices
    )
    backs = [from_behind(block, -offset) for block, offset in zip(rest[:4], offsets)]
    if packed:
        proj_sums = unpack_proj(scatter_shards(*rest[4:], devices), position, width, devices)
    else:
        rest[-1] = rest[-1][0]
        proj_sums = scatter_plain(rest[4:], (0, 0, 0, 1, 0))
    grad_nodes = finish(nodes, gact, backs, send_rows, mod, gmid)
    grad_up, grad_down, grad_out, grad_b_up, grad_b_down = feed_sums
    grad_query, grad_key, grad_value, grad_cond, grad_cond_bias = proj_sums
    return (
        result,
        grad_nodes,
        grad_query,
        grad_key,
        grad_value,
        grad_out,
        grad_up,
        grad_b_up,
        grad_down,
        grad_b_down,
        grad_cond,
        grad_cond_bias,
    )


def solution(mesh):
    both = P(("patch", "sample"), None)
    flat = P(("patch", "sample"))
    split = P("sample", "patch", None)
    cond = P(None, ("patch", "sample"))
    return jax.shard_map(
        body,
        mesh=mesh,
        in_specs=(
            split,
            P("patch", None),
            P("patch", None),
            P("sample", None),
            both,
            both,
            both,
            both,
            both,
            flat,
            both,
            flat,
            cond,
            flat,
            split,
        ),
        out_specs=(split, split, both, both, both, both, both, flat, both, flat, cond, flat),
        check_vma=False,
    )
```

time: 2690 us -> 300 us (0.11)
  waiting for transfers between devices: 865 us -> 92.4 us
  other arithmetic: 696 us -> 8.53 us
  local copies, waits for them, and re-layouts: 460 us -> 21.2 us
  blocking collectives: 421 us -> 0 us
  matrix products: 178 us -> 0 us
  Pallas kernels: 0 us -> 126 us
    reduce_scatter x6 -> x0, waiting for transfers between devices: 825 us -> none  [the longest x1 143 us: body(): lax.psum_scatter(grad_down, ('patch', 'sample'), scatter_dimension=0, til...]
    scatter-add x10 -> x0, other arithmetic: 489 us -> none  [the longest x1 213 us: body(): jax.ops.segment_sum(grad_value_near.reshape(-1, width), slots, num_segmen...]
    all_gather x5 -> x0, blocking collectives: 342 us -> none  [the longest x1 71.3 us: body(): lax.all_gather(w_out, ('patch', 'sample'), axis=0, tiled=True)]
    gather x10 -> x0, local copies, waits for them, and re-layouts: 191 us -> none  [the longest x1 84.5 us: body(): value_table[:, neighbours].reshape(samples, count, -1, heads, HEAD)]
    dot_general x24 -> x0, matrix products: 178 us -> none  [the longest x18 104 us: product(): jnp.dot(left_operand, right_operand, preferred_element_type=jnp.float32)]
    reshape x8 -> x2, local copies, waits for them, and re-layouts: 130 us -> 1.44 us  [the longest x1 0.8 us: prepare(): send_column = send_rows.reshape(ways * each, 1)]
    pallas_call x0 -> x7, Pallas kernels: none -> 126 us  [the longest x1 44.9 us: feed(): pl.pallas_call(feed_kernel, grid=(samples,), in_specs=[smem(), tile, tile...]
    ppermute x16 -> x36, waiting for transfers between devices: 6.32 us -> 92.4 us  [the longest x28 83.8 us: swap(): return lax.ppermute(block, AXES, [(i, i ^ bits) for i in range(devices)])]
  transfers between devices with their start and end apart: 25 -> 36, of which waited for: 10 -> 19; matrix products, arithmetic and copies ran while one was open for 32% -> 6% of each run, Pallas kernels for 0% -> 26%
where the time goes in v1:
time: 300 us
  Pallas kernels  126 us (42%)
  waiting for transfers between devices  92.4 us (31%)
  starting transfers between devices  50.3 us (17%)
  local copies, waits for them, and re-layouts  21.2 us (7%)
  other arithmetic  8.53 us (3%)
    ppermute x28, waiting for transfers between devices, swap(): return lax.ppermute(block, AXES, [(i, i ^ bits) for i in range(devices)])  83.8 us
    pallas_call x1, Pallas kernels, feed(): pl.pallas_call(feed_kernel, grid=(samples,), in_specs=[smem(), tile, tile...  44.9 us
    ppermute x28, starting transfers between devices, swap(): return lax.ppermute(block, AXES, [(i, i ^ bits) for i in range(devices)])  38.2 us
    pallas_call x1, Pallas kernels, attend_back(): pl.pallas_call(attend_back_kernel, grid=(samples,), in_specs=[smem(), til...  31.8 us
    pallas_call x1, Pallas kernels, attend(): pl.pallas_call(attend_kernel, grid=(samples,), in_specs=[per_sample((coun...  23.2 us
    ppermute x8, starting transfers between devices, from_behind(): lax.ppermute(block, 'patch', [((i - distance) % count, i) for i in range(...  12.1 us
    pallas_call x1, Pallas kernels, prepare(): pl.pallas_call(prepare_kernel, out_shape=out, compiler_params=pltpu.Compi...  10.2 us
    unnamed x52, local copies, waits for them, and re-layouts  10.2 us
  transfers between devices with their start and end apart: 36, of which 19 were waited for; matrix products, arithmetic and copies ran while one was open for 6% of the time, Pallas kernels for 26%

profile of v1, /device:TPU:0, one launch (start us, length us, event | category | flops | bytes accessed | tf_op | source)
XLA Modules:
  0.0 299.7 jit_solution(16606111584758673284)
XLA Ops:
  6.6 3.1 %collective-permute-start.11 = (bf16[1,160,512]{2,1,0:T(8,128)(2,1)S(1)}, bf16[1,160,512]{2,1,0:T(8,128)(2,1)S(1)}, u32[]{:S(2)}, u32[]{:S(2)}) collective-permute-start(bf16[1,160,512]{2,1,0:T(8,128)(2,1)S(1)} %bitcast.36), channel_id=1, source_target_pairs={{0,8},{1,9},{2,10},{3,11},{4,12},{5,13},{6,14},{7,15},{8,0},{9,1},... | collective-permute-start | bytes 491528 | tf_op jit(solution)/shard_map/ppermute | solution.py:34
  9.7 2.6 collective-permute-start.12
  12.3 4.1 %collective-permute-done.11 = bf16[1,160,512]{2,1,0:T(8,128)(2,1)S(1)} collective-permute-done((bf16[1,160,512]{2,1,0:T(8,128)(2,1)S(1)}, bf16[1,160,512]{2,1,0:T(8,128)(2,1)S(1)}, u32[]{:S(2)}, u32[]{:S(2)}) %collective-permute-start.11) | collective-permute-done | bytes 163872 | tf_op jit(solution)/shard_map/ppermute | solution.py:34
  16.4 8.3 %collective-permute-done.12 = bf16[1,160,512]{2,1,0:T(8,128)(2,1)S(1)} collective-permute-done((bf16[1,160,512]{2,1,0:T(8,128)(2,1)S(1)}, bf16[1,160,512]{2,1,0:T(8,128)(2,1)S(1)}, u32[]{:S(2)}, u32[]{:S(2)}) %collective-permute-start.12) | collective-permute-done | bytes 163872 | tf_op jit(solution)/shard_map/ppermute | solution.py:34
  28.5 13.1 %collective-permute-done.14 = bf16[4,160,512]{2,1,0:T(8,128)(2,1)S(1)} collective-permute-done((bf16[4,160,512]{2,1,0:T(8,128)(2,1)S(1)}, bf16[4,160,512]{2,1,0:T(8,128)(2,1)S(1)}, u32[]{:S(2)}, u32[]{:S(2)}) %collective-permute-start.14) | collective-permute-done | bytes 655392 | tf_op jit(solution)/shard_map/ppermute | solution.py:34
  41.7 2.4 collective-permute-done.15
  44.1 10.1 %collective-permute-done.16 = bf16[4,160,512]{2,1,0:T(8,128)(2,1)S(1)} collective-permute-done((bf16[4,160,512]{2,1,0:T(8,128)(2,1)S(1)}, bf16[4,160,512]{2,1,0:T(8,128)(2,1)S(1)}, u32[]{:S(2)}, u32[]{:S(2)}) %collective-permute-start.16) | collective-permute-done | bytes 655392 | tf_op jit(solution)/shard_map/ppermute | solution.py:34
  54.6 4.1 %collective-permute-start.4 = (bf16[1,64,512]{2,1,0:T(8,128)(2,1)S(1)}, bf16[1,64,512]{2,1,0:T(8,128)(2,1)S(1)}, u32[]{:S(2)}, u32[]{:S(2)}) collective-permute-start(bf16[1,64,512]{2,1,0:T(8,128)(2,1)S(1)} %fusion.2), channel_id=1, source_target_pairs={{0,8},{1,9},{2,10},{3,11},{4,12},{5,13},{6,14},{7,15},{8,0},{9,1},... | collective-permute-start | bytes 196616 | tf_op jit(solution)/shard_map/ppermute | solution.py:34
  62.0 5.0 %collective-permute-done.5 = bf16[1,64,512]{2,1,0:T(8,128)(2,1)S(1)} collective-permute-done((bf16[1,64,512]{2,1,0:T(8,128)(2,1)S(1)}, bf16[1,64,512]{2,1,0:T(8,128)(2,1)S(1)}, u32[]{:S(2)}, u32[]{:S(2)}) %collective-permute-start.5) | collective-permute-done | bytes 65568 | tf_op jit(solution)/shard_map/ppermute | solution.py:34
  72.5 2.9 collective-permute-done.7
  78.5 2.9 collective-permute-done.9
  82.9 10.2 %shard_map.238 = (f32[768,512]{1,0:T(8,128)}, bf16[4,64,512]{2,1,0:T(8,128)(2,1)}, bf16[4,64,512]{2,1,0:T(8,128)(2,1)}, bf16[4,64,512]{2,1,0:T(8,128)(2,1)}, bf16[4,64,512]{2,1,0:T(8,128)(2,1)}) custom-call(bf16[4,512,512]{2,1,0:T(8,128)(2,1)} %nodes_ref.3, s32[256,1]{1,0:T(8,128)} %reshape.75.send_ref, s32[16,512]{1,0:T(8,128)} %bitcast.40), custom_call_target="tpu_custom_call" | custom-call | tf_op jit(solution)/shard_map/pallas_call | solution.py:141
  93.6 3.9 %collective-permute-start.1 = (bf16[4,64,512]{2,1,0:T(8,128)(2,1)}, bf16[4,64,512]{2,1,0:T(8,128)(2,1)S(1)}, u32[]{:S(2)}, u32[]{:S(2)}) collective-permute-start(bf16[4,64,512]{2,1,0:T(8,128)(2,1)} %get-tuple-element.46), channel_id=1, source_target_pairs={{2,0},{4,2},{6,4},{8,6},{10,8},{12,10},{14,12},{16,14},{18,16},{20... | collective-permute-start | bytes 786440 | tf_op jit(solution)/shard_map/ppermute | solution.py:30
  98.0 3.4 %collective-permute-start.3 = (bf16[4,64,512]{2,1,0:T(8,128)(2,1)}, bf16[4,64,512]{2,1,0:T(8,128)(2,1)}, u32[]{:S(2)}, u32[]{:S(2)}) collective-permute-start(bf16[4,64,512]{2,1,0:T(8,128)(2,1)} %get-tuple-element.48), channel_id=1, source_target_pairs={{8,0},{10,2},{12,4},{14,6},{16,8},{18,10},{20,12},{22,14},{24,16},... | collective-permute-start | bytes 786440 | tf_op jit(solution)/shard_map/ppermute | solution.py:30
  102.1 2.8 shard_map.239
  104.9 5.8 %collective-permute-done.2.refs_3_.refs_4_ = bf16[4,64,512]{2,1,0:T(8,128)(2,1)S(1)} collective-permute-done((bf16[4,64,512]{2,1,0:T(8,128)(2,1)}, bf16[4,64,512]{2,1,0:T(8,128)(2,1)S(1)}, u32[]{:S(2)}, u32[]{:S(2)}) %collective-permute-start.2) | collective-permute-done | bytes 262176 | tf_op jit(solution)/shard_map/ppermute | solution.py:30
  110.7 2.8 collective-permute-done.3.refs_4_.refs_5_
  113.5 23.2 %shard_map.240 = (bf16[4,768,512]{2,1,0:T(8,128)(2,1)}, bf16[4,512,512]{2,1,0:T(8,128)(2,1)}, bf16[4,768,512]{2,1,0:T(8,128)(2,1)}, bf16[4,768,512]{2,1,0:T(8,12...) custom-call(bf16[4,512,512]{2,1,0:T(8,128)(2,1)} %nodes_ref.3, bf16[4,64,512]{2,1,0:T(8,128)(2,1)} %copy-done.3, ...), custom_call_target="tpu_custom_call" | custom-call | tf_op jit(solution)/shard_map/pallas_call | solution.py:331
  136.7 4.8 %shard_map.241 = (bf16[512,512]{1,0:T(8,128)(2,1)}, bf16[512,2048]{1,0:T(8,128)(2,1)}, bf16[2048,512]{1,0:T(8,128)(2,1)}, f32[1,2048]{1,0:T(1,128)}, f32[1,512]{1,0:T(1,128)}) custom-call(s32[1]{0:T(128)} %bitcast.me_ref.refs_0_, bf16[16,160,512]{2,1,0:T(8,128)(2,1)} %copy-done, bf16[16,160,512]{2,1,0:T(8,128)(2,1)} %collective-permute-done.17.high_ref), custom_call_target="tpu_custom_call" | custom-call | tf_op jit(solution)/shard_map/pallas_call | solution.py:274
  141.6 44.9 %shard_map.242 = (bf16[4,512,512]{2,1,0:T(8,128)(2,1)}, f32[4,512,512]{2,1,0:T(8,128)}, bf16[4,512,512]{2,1,0:T(8,128)(2,1)}, f32[4,2,512]{2,1,0:T(2,128)}, bf16...) custom-call(s32[1]{0:T(128)} %bitcast.me_ref.refs_0_, bf16[4,512,512]{2,1,0:T(8,128)(2,1)} %nodes_ref.3, ...), custom_call_target="tpu_custom_call" | custom-call | tf_op jit(solution)/shard_map/pallas_call | solution.py:457
  187.2 31.8 %shard_map.243 = (f32[4,512,512]{2,1,0:T(8,128)}, bf16[4,64,512]{2,1,0:T(8,128)(2,1)}, bf16[4,64,512]{2,1,0:T(8,128)(2,1)}, bf16[4,64,512]{2,1,0:T(8,128)(2,1)},...) custom-call(s32[1]{0:T(128)} %bitcast.me_ref.refs_0_, ...), custom_call_target="tpu_custom_call" | custom-call | tf_op jit(solution)/shard_map/pallas_call | solution.py:584
  219.7 2.5 collective-permute-done.22
  228.8 3.8 %collective-permute-done.23 = bf16[4,64,512]{2,1,0:T(8,128)(2,1)S(1)} collective-permute-done((bf16[4,64,512]{2,1,0:T(8,128)(2,1)S(1)}, bf16[4,64,512]{2,1,0:T(8,128)(2,1)S(1)}, u32[]{:S(2)}, u32[]{:S(2)}) %collective-permute-start.23) | collective-permute-done | bytes 262176 | tf_op jit(solution)/shard_map/ppermute | solution.py:34
  232.6 2.7 collective-permute-done.24
  237.4 4.8 %collective-permute-done.25 = bf16[4,64,512]{2,1,0:T(8,128)(2,1)S(1)} collective-permute-done((bf16[4,64,512]{2,1,0:T(8,128)(2,1)S(1)}, bf16[4,64,512]{2,1,0:T(8,128)(2,1)S(1)}, u32[]{:S(2)}, u32[]{:S(2)}) %collective-permute-start.25) | collective-permute-done | bytes 262176 | tf_op jit(solution)/shard_map/ppermute | solution.py:34
  244.4 2.6 add_convert_fusion
  254.2 2.1 collective-permute-start.27
  257.6 2.6 collective-permute-start.28
  260.8 8.5 %shard_map.244 = f32[4,512,512]{2,1,0:T(8,128)} custom-call(bf16[4,512,512]{2,1,0:T(8,128)(2,1)} %nodes_ref.3, f32[4,512,512]{2,1,0:T(8,128)} %get-tuple-element.68.gact_ref, bf16[4,64,512]{2,1,0:T(8,128)(2,1)} %collective-permute-done.18.b0, bf16[4,64,512]{2,1,0:T(8,128)(2,1)} %collective-permute-done.19.b1, ...), custom_call_target="tpu_custom_call" | custom-call | tf_op jit(solution)/shard_map/pallas_call | solution.py:629
  270.9 8.6 %collective-permute-done.32 = bf16[4,160,512]{2,1,0:T(8,128)(2,1)} collective-permute-done((bf16[4,160,512]{2,1,0:T(8,128)(2,1)}, bf16[4,160,512]{2,1,0:T(8,128)(2,1)}, u32[]{:S(2)}, u32[]{:S(2)}) %collective-permute-start.32) | collective-permute-done | bytes 655392 | tf_op jit(solution)/shard_map/ppermute | solution.py:34
  281.2 2.1 collective-permute-start.33
  287.8 8.7 %collective-permute-done.34 = bf16[1,160,512]{2,1,0:T(8,128)(2,1)S(1)} collective-permute-done((bf16[1,160,512]{2,1,0:T(8,128)(2,1)S(1)}, bf16[1,160,512]{2,1,0:T(8,128)(2,1)S(1)}, u32[]{:S(2)}, u32[]{:S(2)}) %collective-permute-start.34) | collective-permute-done | bytes 163872 | tf_op jit(solution)/shard_map/ppermute | solution.py:34
  (139 shorter events, 57.4 us)
Async XLA Ops:
  6.6 9.8 %collective-permute-start.11 = (bf16[1,160,512]{2,1,0:T(8,128)(2,1)S(1)}, bf16[1,160,512]{2,1,0:T(8,128)(2,1)S(1)}, u32[]{:S(2)}, u32[]{:S(2)}) collective-permute-start(bf16[1,160,512]{2,1,0:T(8,128)(2,1)S(1)} %bitcast.36), channel_id=1, source_target_pairs={{0,8},{1,9},{2,10},{3,11},{4,12},{5,13},{6,14},{7,15},{8,0},{9,1},... | collective-permute-start | bytes 491528 | tf_op jit(solution)/shard_map/ppermute | solution.py:34
  9.7 15.0 %collective-permute-start.12 = (bf16[1,160,512]{2,1,0:T(8,128)(2,1)S(1)}, bf16[1,160,512]{2,1,0:T(8,128)(2,1)S(1)}, u32[]{:S(2)}, u32[]{:S(2)}) collective-permute-start(bf16[1,160,512]{2,1,0:T(8,128)(2,1)S(1)} %bitcast.37), channel_id=1, source_target_pairs={{0,16},{1,17},{2,18},{3,19},{4,20},{5,21},{6,22},{7,23},{8,24},{9,... | collective-permute-start | bytes 491528 | tf_op jit(solution)/shard_map/ppermute | solution.py:34
  12.3 12.4 %collective-permute-start.13 = (bf16[1,160,512]{2,1,0:T(8,128)(2,1)S(1)}, bf16[1,160,512]{2,1,0:T(8,128)(2,1)S(1)}, u32[]{:S(2)}, u32[]{:S(2)}) collective-permute-start(bf16[1,160,512]{2,1,0:T(8,128)(2,1)S(1)} %bitcast.38), channel_id=1, source_target_pairs={{0,24},{1,25},{2,26},{3,27},{4,28},{5,29},{6,30},{7,31},{8,16},{9,... | collective-permute-start | bytes 491528 | tf_op jit(solution)/shard_map/ppermute | solution.py:34
  24.9 16.8 %collective-permute-start.14 = (bf16[4,160,512]{2,1,0:T(8,128)(2,1)S(1)}, bf16[4,160,512]{2,1,0:T(8,128)(2,1)S(1)}, u32[]{:S(2)}, u32[]{:S(2)}) collective-permute-start(bf16[4,160,512]{2,1,0:T(8,128)(2,1)S(1)} %pad_maximum_fusion), channel_id=1, source_target_pairs={{0,1},{1,0},{2,3},{3,2},{4,5},{5,4},{6,7},{7,6},{8,9},{9,8},{10,11... | collective-permute-start | bytes 1966088 | tf_op jit(solution)/shard_map/ppermute | solution.py:34
  26.4 17.6 %collective-permute-start.15 = (bf16[4,160,512]{2,1,0:T(8,128)(2,1)S(1)}, bf16[4,160,512]{2,1,0:T(8,128)(2,1)S(1)}, u32[]{:S(2)}, u32[]{:S(2)}) collective-permute-start(bf16[4,160,512]{2,1,0:T(8,128)(2,1)S(1)} %pad_maximum_fusion), channel_id=1, source_target_pairs={{0,4},{1,5},{2,6},{3,7},{4,0},{5,1},{6,2},{7,3},{8,12},{9,13},{10,... | collective-permute-start | bytes 1966088 | tf_op jit(solution)/shard_map/ppermute | solution.py:34
  27.9 26.3 %collective-permute-start.16 = (bf16[4,160,512]{2,1,0:T(8,128)(2,1)S(1)}, bf16[4,160,512]{2,1,0:T(8,128)(2,1)S(1)}, u32[]{:S(2)}, u32[]{:S(2)}) collective-permute-start(bf16[4,160,512]{2,1,0:T(8,128)(2,1)S(1)} %pad_maximum_fusion), channel_id=1, source_target_pairs={{0,5},{1,4},{2,7},{3,6},{4,1},{5,0},{6,3},{7,2},{8,13},{9,12},{10,... | collective-permute-start | bytes 1966088 | tf_op jit(solution)/shard_map/ppermute | solution.py:34
  54.3 82.4 %collective-permute-start.17 = (bf16[16,160,512]{2,1,0:T(8,128)(2,1)S(1)}, bf16[16,160,512]{2,1,0:T(8,128)(2,1)}, u32[]{:S(2)}, u32[]{:S(2)}) collective-permute-start(bf16[16,160,512]{2,1,0:T(8,128)(2,1)S(1)} %constant_dynamic-update-slice_fusion.14.low_ref), channel_id=1, source_target_pairs={{0,2},{1,3},{2,0},{3,1},{4,6},{5,7},{6,4},{7,5},{8,10},{9,11},{10,... | collective-permute-start | bytes 7864328 | tf_op jit(solution)/shard_map/ppermute | solution.py:34
  54.6 7.3 %collective-permute-start.4 = (bf16[1,64,512]{2,1,0:T(8,128)(2,1)S(1)}, bf16[1,64,512]{2,1,0:T(8,128)(2,1)S(1)}, u32[]{:S(2)}, u32[]{:S(2)}) collective-permute-start(bf16[1,64,512]{2,1,0:T(8,128)(2,1)S(1)} %fusion.2), channel_id=1, source_target_pairs={{0,8},{1,9},{2,10},{3,11},{4,12},{5,13},{6,14},{7,15},{8,0},{9,1},... | collective-permute-start | bytes 196616 | tf_op jit(solution)/shard_map/ppermute | solution.py:34
  58.7 8.3 %collective-permute-start.5 = (bf16[1,64,512]{2,1,0:T(8,128)(2,1)S(1)}, bf16[1,64,512]{2,1,0:T(8,128)(2,1)S(1)}, u32[]{:S(2)}, u32[]{:S(2)}) collective-permute-start(bf16[1,64,512]{2,1,0:T(8,128)(2,1)S(1)} %fusion.2), channel_id=1, source_target_pairs={{0,16},{1,17},{2,18},{3,19},{4,20},{5,21},{6,22},{7,23},{8,24},{9,... | collective-permute-start | bytes 196616 | tf_op jit(solution)/shard_map/ppermute | solution.py:34
  67.0 8.3 %collective-permute-start.7 = (bf16[4,64,512]{2,1,0:T(8,128)(2,1)S(1)}, bf16[4,64,512]{2,1,0:T(8,128)(2,1)S(1)}, u32[]{:S(2)}, u32[]{:S(2)}) collective-permute-start(bf16[4,64,512]{2,1,0:T(8,128)(2,1)S(1)} %pad_maximum_fusion.1), channel_id=1, source_target_pairs={{0,1},{1,0},{2,3},{3,2},{4,5},{5,4},{6,7},{7,6},{8,9},{9,8},{10,11... | collective-permute-start | bytes 786440 | tf_op jit(solution)/shard_map/ppermute | solution.py:34
  68.6 9.2 %collective-permute-start.8 = (bf16[4,64,512]{2,1,0:T(8,128)(2,1)S(1)}, bf16[4,64,512]{2,1,0:T(8,128)(2,1)S(1)}, u32[]{:S(2)}, u32[]{:S(2)}) collective-permute-start(bf16[4,64,512]{2,1,0:T(8,128)(2,1)S(1)} %pad_maximum_fusion.1), channel_id=1, source_target_pairs={{0,4},{1,5},{2,6},{3,7},{4,0},{5,1},{6,2},{7,3},{8,12},{9,13},{10,... | collective-permute-start | bytes 786440 | tf_op jit(solution)/shard_map/ppermute | solution.py:34
  70.1 11.3 %collective-permute-start.9 = (bf16[4,64,512]{2,1,0:T(8,128)(2,1)S(1)}, bf16[4,64,512]{2,1,0:T(8,128)(2,1)S(1)}, u32[]{:S(2)}, u32[]{:S(2)}) collective-permute-start(bf16[4,64,512]{2,1,0:T(8,128)(2,1)S(1)} %pad_maximum_fusion.1), channel_id=1, source_target_pairs={{0,5},{1,4},{2,7},{3,6},{4,1},{5,0},{6,3},{7,2},{8,13},{9,12},{10,... | collective-permute-start | bytes 786440 | tf_op jit(solution)/shard_map/ppermute | solution.py:34
  82.1 15.9 %collective-permute-start.10 = (bf16[16,64,512]{2,1,0:T(8,128)(2,1)}, bf16[16,64,512]{2,1,0:T(8,128)(2,1)}, u32[]{:S(2)}, u32[]{:S(2)}) collective-permute-start(bf16[16,64,512]{2,1,0:T(8,128)(2,1)} %constant_dynamic-update-slice_fusion.low_ref), channel_id=1, source_target_pairs={{0,2},{1,3},{2,0},{3,1},{4,6},{5,7},{6,4},{7,5},{8,10},{9,11},{10,... | collective-permute-start | bytes 3145736 | tf_op jit(solution)/shard_map/ppermute | solution.py:34
  93.1 11.7 %collective-permute-start = (bf16[4,64,512]{2,1,0:T(8,128)(2,1)}, bf16[4,64,512]{2,1,0:T(8,128)(2,1)S(1)}, u32[]{:S(2)}, u32[]{:S(2)}) collective-permute-start(bf16[4,64,512]{2,1,0:T(8,128)(2,1)} %get-tuple-element.45), channel_id=1, source_target_pairs={{30,0},{0,2},{2,4},{4,6},{6,8},{8,10},{10,12},{12,14},{14,16},{16,... | collective-permute-start | bytes 786440 | tf_op jit(solution)/shard_map/ppermute | solution.py:30
  93.6 11.3 %collective-permute-start.1 = (bf16[4,64,512]{2,1,0:T(8,128)(2,1)}, bf16[4,64,512]{2,1,0:T(8,128)(2,1)S(1)}, u32[]{:S(2)}, u32[]{:S(2)}) collective-permute-start(bf16[4,64,512]{2,1,0:T(8,128)(2,1)} %get-tuple-element.46), channel_id=1, source_target_pairs={{2,0},{4,2},{6,4},{8,6},{10,8},{12,10},{14,12},{16,14},{18,16},{20... | collective-permute-start | bytes 786440 | tf_op jit(solution)/shard_map/ppermute | solution.py:30
  97.6 13.1 %collective-permute-start.2 = (bf16[4,64,512]{2,1,0:T(8,128)(2,1)}, bf16[4,64,512]{2,1,0:T(8,128)(2,1)S(1)}, u32[]{:S(2)}, u32[]{:S(2)}) collective-permute-start(bf16[4,64,512]{2,1,0:T(8,128)(2,1)} %get-tuple-element.47), channel_id=1, source_target_pairs={{24,0},{26,2},{28,4},{30,6},{0,8},{2,10},{4,12},{6,14},{8,16},{10,... | collective-permute-start | bytes 786440 | tf_op jit(solution)/shard_map/ppermute | solution.py:30
  98.0 15.5 %collective-permute-start.3 = (bf16[4,64,512]{2,1,0:T(8,128)(2,1)}, bf16[4,64,512]{2,1,0:T(8,128)(2,1)}, u32[]{:S(2)}, u32[]{:S(2)}) collective-permute-start(bf16[4,64,512]{2,1,0:T(8,128)(2,1)} %get-tuple-element.48), channel_id=1, source_target_pairs={{8,0},{10,2},{12,4},{14,6},{16,8},{18,10},{20,12},{22,14},{24,16},... | collective-permute-start | bytes 786440 | tf_op jit(solution)/shard_map/ppermute | solution.py:30
  186.4 56.5 %collective-permute-start.29 = (bf16[16,160,512]{2,1,0:T(8,128)(2,1)}, bf16[16,160,512]{2,1,0:T(8,128)(2,1)S(1)}, u32[]{:S(2)}, u32[]{:S(2)}) collective-permute-start(bf16[16,160,512]{2,1,0:T(8,128)(2,1)} %get-tuple-element.77), channel_id=1, source_target_pairs={{0,2},{1,3},{2,0},{3,1},{4,6},{5,7},{6,4},{7,5},{8,10},{9,11},{10,... | collective-permute-start | bytes 7864328 | tf_op jit(solution)/shard_map/ppermute | solution.py:34
  223.9 8.7 %collective-permute-start.23 = (bf16[4,64,512]{2,1,0:T(8,128)(2,1)S(1)}, bf16[4,64,512]{2,1,0:T(8,128)(2,1)S(1)}, u32[]{:S(2)}, u32[]{:S(2)}) collective-permute-start(bf16[4,64,512]{2,1,0:T(8,128)(2,1)S(1)} %get-tuple-element.81), channel_id=1, source_target_pairs={{0,1},{1,0},{2,3},{3,2},{4,5},{5,4},{6,7},{7,6},{8,9},{9,8},{10,11... | collective-permute-start | bytes 786440 | tf_op jit(solution)/shard_map/ppermute | solution.py:34
  225.5 9.8 %collective-permute-start.24 = (bf16[4,64,512]{2,1,0:T(8,128)(2,1)S(1)}, bf16[4,64,512]{2,1,0:T(8,128)(2,1)S(1)}, u32[]{:S(2)}, u32[]{:S(2)}) collective-permute-start(bf16[4,64,512]{2,1,0:T(8,128)(2,1)S(1)} %get-tuple-element.83), channel_id=1, source_target_pairs={{0,4},{1,5},{2,6},{3,7},{4,0},{5,1},{6,2},{7,3},{8,12},{9,13},{10,... | collective-permute-start | bytes 786440 | tf_op jit(solution)/shard_map/ppermute | solution.py:34
  225.8 16.4 %collective-permute-start.25 = (bf16[4,64,512]{2,1,0:T(8,128)(2,1)S(1)}, bf16[4,64,512]{2,1,0:T(8,128)(2,1)S(1)}, u32[]{:S(2)}, u32[]{:S(2)}) collective-permute-start(bf16[4,64,512]{2,1,0:T(8,128)(2,1)S(1)} %get-tuple-element.82), channel_id=1, source_target_pairs={{0,5},{1,4},{2,7},{3,6},{4,1},{5,0},{6,3},{7,2},{8,13},{9,12},{10,... | collective-permute-start | bytes 786440 | tf_op jit(solution)/shard_map/ppermute | solution.py:34
  227.5 22.4 %collective-permute-start.18 = (bf16[4,64,512]{2,1,0:T(8,128)(2,1)S(1)}, bf16[4,64,512]{2,1,0:T(8,128)(2,1)}, u32[]{:S(2)}, u32[]{:S(2)}) collective-permute-start(bf16[4,64,512]{2,1,0:T(8,128)(2,1)S(1)} %copy-done.15), channel_id=1, source_target_pairs={{2,0},{4,2},{6,4},{8,6},{10,8},{12,10},{14,12},{16,14},{18,16},{20... | collective-permute-start | bytes 786440 | tf_op jit(solution)/shard_map/ppermute | solution.py:30
  232.6 18.4 %collective-permute-start.19 = (bf16[4,64,512]{2,1,0:T(8,128)(2,1)S(1)}, bf16[4,64,512]{2,1,0:T(8,128)(2,1)}, u32[]{:S(2)}, u32[]{:S(2)}) collective-permute-start(bf16[4,64,512]{2,1,0:T(8,128)(2,1)S(1)} %copy-done.14), channel_id=1, source_target_pairs={{30,0},{0,2},{2,4},{4,6},{6,8},{8,10},{10,12},{12,14},{14,16},{16,... | collective-permute-start | bytes 786440 | tf_op jit(solution)/shard_map/ppermute | solution.py:30
  235.3 17.2 %collective-permute-start.20 = (bf16[4,64,512]{2,1,0:T(8,128)(2,1)S(1)}, bf16[4,64,512]{2,1,0:T(8,128)(2,1)}, u32[]{:S(2)}, u32[]{:S(2)}) collective-permute-start(bf16[4,64,512]{2,1,0:T(8,128)(2,1)S(1)} %copy-done.13), channel_id=1, source_target_pairs={{8,0},{10,2},{12,4},{14,6},{16,8},{18,10},{20,12},{22,14},{24,16},... | collective-permute-start | bytes 786440 | tf_op jit(solution)/shard_map/ppermute | solution.py:30
  242.2 12.0 %collective-permute-start.21 = (bf16[4,64,512]{2,1,0:T(8,128)(2,1)S(1)}, bf16[4,64,512]{2,1,0:T(8,128)(2,1)}, u32[]{:S(2)}, u32[]{:S(2)}) collective-permute-start(bf16[4,64,512]{2,1,0:T(8,128)(2,1)S(1)} %copy-done.12), channel_id=1, source_target_pairs={{24,0},{26,2},{28,4},{30,6},{0,8},{2,10},{4,12},{6,14},{8,16},{10,... | collective-permute-start | bytes 786440 | tf_op jit(solution)/shard_map/ppermute | solution.py:30
  248.4 22.5 %collective-permute-start.30 = (bf16[4,160,512]{2,1,0:T(8,128)(2,1)}, bf16[4,160,512]{2,1,0:T(8,128)(2,1)S(1)}, u32[]{:S(2)}, u32[]{:S(2)}) collective-permute-start(bf16[4,160,512]{2,1,0:T(8,128)(2,1)} %get-tuple-element.78), channel_id=1, source_target_pairs={{0,1},{1,0},{2,3},{3,2},{4,5},{5,4},{6,7},{7,6},{8,9},{9,8},{10,11... | collective-permute-start | bytes 1966088 | tf_op jit(solution)/shard_map/ppermute | solution.py:34
  249.9 21.0 %collective-permute-start.31 = (bf16[4,160,512]{2,1,0:T(8,128)(2,1)}, bf16[4,160,512]{2,1,0:T(8,128)(2,1)}, u32[]{:S(2)}, u32[]{:S(2)}) collective-permute-start(bf16[4,160,512]{2,1,0:T(8,128)(2,1)} %get-tuple-element.80), channel_id=1, source_target_pairs={{0,4},{1,5},{2,6},{3,7},{4,0},{5,1},{6,2},{7,3},{8,12},{9,13},{10,... | collective-permute-start | bytes 1966088 | tf_op jit(solution)/shard_map/ppermute | solution.py:34
  251.0 28.5 %collective-permute-start.32 = (bf16[4,160,512]{2,1,0:T(8,128)(2,1)}, bf16[4,160,512]{2,1,0:T(8,128)(2,1)}, u32[]{:S(2)}, u32[]{:S(2)}) collective-permute-start(bf16[4,160,512]{2,1,0:T(8,128)(2,1)} %get-tuple-element.79), channel_id=1, source_target_pairs={{0,5},{1,4},{2,7},{3,6},{4,1},{5,0},{6,3},{7,2},{8,13},{9,12},{10,... | collective-permute-start | bytes 1966088 | tf_op jit(solution)/shard_map/ppermute | solution.py:34
  254.2 15.1 %collective-permute-start.27 = (bf16[1,64,512]{2,1,0:T(8,128)(2,1)}, bf16[1,64,512]{2,1,0:T(8,128)(2,1)}, u32[]{:S(2)}, u32[]{:S(2)}) collective-permute-start(bf16[1,64,512]{2,1,0:T(8,128)(2,1)} %get-tuple-element.96), channel_id=1, source_target_pairs={{0,16},{1,17},{2,18},{3,19},{4,20},{5,21},{6,22},{7,23},{8,24},{9,... | collective-permute-start | bytes 196616 | tf_op jit(solution)/shard_map/ppermute | solution.py:34
  257.6 11.7 %collective-permute-start.28 = (bf16[1,64,512]{2,1,0:T(8,128)(2,1)}, bf16[1,64,512]{2,1,0:T(8,128)(2,1)}, u32[]{:S(2)}, u32[]{:S(2)}) collective-permute-start(bf16[1,64,512]{2,1,0:T(8,128)(2,1)} %get-tuple-element.95), channel_id=1, source_target_pairs={{0,24},{1,25},{2,26},{3,27},{4,28},{5,29},{6,30},{7,31},{8,16},{9,... | collective-permute-start | bytes 196616 | tf_op jit(solution)/shard_map/ppermute | solution.py:34
  283.2 13.2 %collective-permute-start.34 = (bf16[1,160,512]{2,1,0:T(8,128)(2,1)S(1)}, bf16[1,160,512]{2,1,0:T(8,128)(2,1)S(1)}, u32[]{:S(2)}, u32[]{:S(2)}) collective-permute-start(bf16[1,160,512]{2,1,0:T(8,128)(2,1)S(1)} %get-tuple-element.86), channel_id=1, source_target_pairs={{0,16},{1,17},{2,18},{3,19},{4,20},{5,21},{6,22},{7,23},{8,24},{9,... | collective-permute-start | bytes 491528 | tf_op jit(solution)/shard_map/ppermute | solution.py:34
  284.8 11.6 %collective-permute-start.35 = (bf16[1,160,512]{2,1,0:T(8,128)(2,1)S(1)}, bf16[1,160,512]{2,1,0:T(8,128)(2,1)S(1)}, u32[]{:S(2)}, u32[]{:S(2)}) collective-permute-start(bf16[1,160,512]{2,1,0:T(8,128)(2,1)S(1)} %get-tuple-element.85), channel_id=1, source_target_pairs={{0,24},{1,25},{2,26},{3,27},{4,28},{5,29},{6,30},{7,31},{8,16},{9,... | collective-permute-start | bytes 491528 | tf_op jit(solution)/shard_map/ppermute | solution.py:34
  (21 other events, 413.6 us)
